TPU v7x, 32 devices: a whole 2x2x4 slice. The times are simulated.
32 devices in a mesh: lat: 4 (over z), lon: 8 (over y, x, core).
Axes of the slice: x: 2, y: 2, z: 4, core: 2. Of those that a mesh axis runs over, the one named last changes fastest.
Arguments:
- samples: bfloat16 [256, 90112], P(None, ('lat', 'lon')), may hold values from -6 to 6
- area_weight: float32 [90112], P(('lat', 'lon')), may hold values from 0.1 to 1
- ocean_count: int32 [4, 8], P('lat', 'lon'), may hold values from 704 to 2816, as said below
- omega: bfloat16 [512, 256], replicated, may hold values from -5 to 5
Outputs:
- point_basis: bfloat16 [512, 90112], P(None, ('lat', 'lon'))
- sample_basis: float32 [8, 256, 64], replicated
Inputs may be any that keep to these rules, and one draw needn't show every extreme that they name: Each device's block of grid points starts with ocean_count ocean points, the rest are land; some device's block is all ocean (2816).
All inputs are finite; a program needn't handle non-finite values.
Results may differ from a plain program's by a relative error of at most 0.0075.
Values sent between devices are 32-bit elements; how exact they have to be, the bound alone decides.
No kernel may reach another device: no remote copies, remote signals or barrier semaphores. Data moves between devices by JAX's collectives and lax.ppermute only.
A program may use at most 64 MiB of HBM per device.

v0:
```python
import jax
import jax.numpy as jnp
from jax import lax
from jax.sharding import PartitionSpec as P

SAMPLES = 256
COLUMNS = 64
FOLDS = 8


def grid_total(partial_value):
    return lax.psum(partial_value, ("lat", "lon"))


def on_device(samples, area_weight, ocean_count, omega):
    point_cols = samples.shape[1]
    fold_row = lax.iota(jnp.int32, FOLDS * COLUMNS) // COLUMNS
    fold_col = lax.iota(jnp.int32, SAMPLES) // (SAMPLES // FOLDS)
    keeping = fold_row[:, None] != fold_col[None, :]
    live = jnp.where(keeping, omega, jnp.zeros_like(omega))
    valid = lax.iota(jnp.int32, point_cols) < ocean_count[0, 0]
    weighted = jnp.where(
        valid[None, :], samples.astype(jnp.float32) * area_weight[None, :], jnp.float32(0.0)
    ).astype(jnp.bfloat16)
    product = jnp.dot(live, weighted, preferred_element_type=jnp.float32)
    scores = product.astype(jnp.bfloat16)
    folded = scores.reshape(FOLDS, COLUMNS, point_cols)
    devices_all = lax.axis_size("lat") * lax.axis_size("lon")
    total = point_cols * devices_all
    exact = product.reshape(FOLDS, COLUMNS, point_cols)
    partial_gram = jnp.einsum("fkp,fjp->fkj", exact, exact, precision=lax.Precision.HIGHEST)
    gram = grid_total(partial_gram)
    partial_cross = jnp.einsum(
        "sp,fkp->fsk", weighted.astype(jnp.float32), exact, precision=lax.Precision.HIGHEST
    )
    lower_factor = jnp.linalg.cholesky(gram)
    identity = jnp.broadcast_to(jnp.eye(COLUMNS, dtype=jnp.float32), (FOLDS, COLUMNS, COLUMNS))
    inverse = jax.scipy.linalg.solve_triangular(lower_factor, identity, lower=True)
    point_scale = (inverse * jnp.float32(total**0.5)).astype(jnp.bfloat16)
    point_basis = jnp.einsum(
        "fkj,fjp->fkp", point_scale, folded, preferred_element_type=jnp.float32
    )
    point_basis = point_basis.astype(jnp.bfloat16).reshape(FOLDS * COLUMNS, point_cols)
    sample_scale = inverse * jnp.float32((SAMPLES / total) ** 0.5)
    cross = lax.psum(partial_cross, ("lat", "lon"))
    sample_basis = jnp.einsum("fsj,fkj->fsk", cross, sample_scale, precision=lax.Precision.HIGHEST)
    return (point_basis, sample_basis)


def solution(mesh):
    in_specs = (P(None, ("lat", "lon")), P(("lat", "lon")), P("lat", "lon"), P())
    out_specs = (P(None, ("lat", "lon")), P())
    return jax.shard_map(
        on_device, mesh=mesh, in_specs=in_specs, out_specs=out_specs, check_vma=False
    )
```

profile of v0, /device:TPU:0, one launch (start us, length us, event | category | flops | bytes accessed | tf_op | source)
XLA Modules:
  0.0 253.4 jit_solution(10656014839347430208)
XLA Ops:
  7.2 0.0 all-reduce.3.cloned.1.call-start
  7.9 0.0 copy-start
  7.9 0.0 copy-start.1
  7.9 2.5 fusion.26
  10.4 0.0 copy-done
  10.4 0.0 copy-done.1
  10.4 3.7 %fusion.2 = f32[8,256,64]{1,2,0:T(8,128)} fusion(f32[8,64,2816]{2,1,0:T(8,128)S(1)} %bitcast.26, bf16[256,2816]{1,0:T(8,128)(2,1)S(1)} %copy-done, f32[2816]{0:T(1024)S(1)} %copy-done.1, pred[2816]{0:T(1024)(128)(4,1)S(1)} %iota_compare_fusion.2), kind=kOutput, calls=%fused_computation.4 | convolution fusion | flops 4432068608 | bytes 7747328 | tf_op jit(solution)/shard_map/sp,fkp->fsk/dot_general | solution.py:33
  14.1 5.9 %fusion.27 = f32[8,64,64]{1,2,0:T(8,128)} fusion(f32[8,64,2816]{2,1,0:T(8,128)S(1)} %bitcast.27), kind=kOutput, calls=%fused_computation.44 | convolution fusion | flops 1107296256 | bytes 5898240 | tf_op jit(solution)/shard_map/fkp,fjp->fkj/dot_general | solution.py:31
  20.0 0.0 all-reduce.3.cloned.1.call-update
  20.0 132.2 %all-reduce.3.cloned.1.call-done = (f32[8,64,64]{1,2,0:T(8,128)}, f32[8,256,64]{1,2,0:T(8,128)}) async-done(((f32[8,64,64]{1,2,0:T(8,128)}, f32[8,256,64]{1,2,0:T(8,128)}), (f32[8,64,64]{1,2,0:T(8,128)}, f32[8,256,64]{1,2,0:T(8,128)})) %all-reduce.3.cloned.1.call-update) | async-done | bytes 655376 | tf_op jit(solution)/shard_map/psum | solution.py:12
  152.3 1.1 copy.10
  153.4 1.0 fusion.8
  154.3 47.1 %custom-call.8 = f32[8,64,64]{2,1,0:T(8,128)S(1)} custom-call(f32[8,64,64]{2,1,0:T(8,128)S(1)} %fusion.8), custom_call_target="Cholesky" | custom-call | tf_op jit(solution)/shard_map/jit(cholesky)/cholesky | solution.py:36
  201.5 0.1 compare_reduce_fusion
  201.6 0.1 select_bitcast_fusion
  201.7 39.3 %custom-call.9 = f32[8,1,64,64]{2,3,1,0:T(8,128)S(1)} custom-call(f32[8,1,64,64]{3,2,1,0:T(8,128)S(1)} %select_bitcast_fusion), custom_call_target="InvertDiagBlocksLowerTriangular" | custom-call | tf_op jit(solution)/shard_map/jit(_solve_triangular)/vmap()/triangular_solve | solution.py:38
  241.0 0.6 fusion.6
  241.6 2.4 fusion.9
  244.1 2.5 convolution_convert_fusion
  (7 shorter events, 0.1 us)
Async XLA Ops:
  7.2 145.1 %all-reduce.3.cloned.1.call-start = ((), (), s32[]{:S(2)}) async-start(), calls=%async_computation | async-start | bytes 1572864 | tf_op jit(solution)/shard_map/psum | solution.py:12
  7.9 2.5 copy-start
  7.9 2.5 copy-start.1
Sparse Core Ops, SparseCore 0:
  20.1 132.1 all-reduce.2
where the time goes:
time: 254 us; the launch traced here: 253 us
  waiting for transfers between devices  132 us (52%)
  other arithmetic  87.7 us (35%)
  matrix products  17.5 us (7%)
  between operations  14.8 us (6%)
    psum x1, waiting for transfers between devices, grid_total(): return lax.psum(partial_value, ('lat', 'lon'))  132 us
    another operation x4, other arithmetic, on_device(): lower_factor = jnp.linalg.cholesky(gram)  47.2 us
    another operation x3, other arithmetic, on_device(): jax.scipy.linalg.solve_triangular(lower_factor, identity, lower=True)  39.4 us
    dot_general x1, matrix products, on_device(): jnp.einsum('fkp,fjp->fkj', exact, exact, precision=lax.Precision.HIGHEST)  5.85 us
  transfers between devices with their start and end apart: 1, of which 1 were waited for; matrix products, arithmetic and copies ran while one was open for 0% of the time, Pallas kernels for 0%

commit v1 on v0

v1 whole, which is shorter than its diff:
```python
import jax
import jax.numpy as jnp
from jax import lax
from jax.sharding import PartitionSpec as P

SAMPLES = 256
COLUMNS = 64
FOLDS = 8
AXES = ("lat", "lon")


def grid_total(value):
    lon = lax.axis_size("lon")
    devices = lax.axis_size("lat") * lon
    if devices & (devices - 1):
        return lax.psum(value, AXES)
    bit = 1
    while bit < devices:
        pairs = [(d, d ^ bit) for d in range(devices)]
        value = value + lax.ppermute(value, AXES, pairs)
        bit *= 2
    return value


def on_device(samples, area_weight, ocean_count, omega):
    point_cols = samples.shape[1]
    fold_row = lax.iota(jnp.int32, FOLDS * COLUMNS) // COLUMNS
    fold_col = lax.iota(jnp.int32, SAMPLES) // (SAMPLES // FOLDS)
    keeping = fold_row[:, None] != fold_col[None, :]
    live = jnp.where(keeping, omega, jnp.zeros_like(omega))
    valid = lax.iota(jnp.int32, point_cols) < ocean_count[0, 0]
    weighted = jnp.where(
        valid[None, :], samples.astype(jnp.float32) * area_weight[None, :], jnp.float32(0.0)
    ).astype(jnp.bfloat16)
    partial_cov = jnp.einsum("sp,tp->st", weighted, weighted, preferred_element_type=jnp.float32)
    cov = grid_total(partial_cov)
    product = jnp.dot(live, weighted, preferred_element_type=jnp.float32)
    scores = product.astype(jnp.bfloat16)
    folded = scores.reshape(FOLDS, COLUMNS, point_cols)
    devices_all = lax.axis_size("lat") * lax.axis_size("lon")
    total = point_cols * devices_all
    live_f = live.astype(jnp.float32).reshape(FOLDS, COLUMNS, SAMPLES)
    cross = jnp.einsum("st,fkt->fsk", cov, live_f, precision=lax.Precision.HIGHEST)
    gram = jnp.einsum("fks,fsj->fkj", live_f, cross, precision=lax.Precision.HIGHEST)
    lower_factor = jnp.linalg.cholesky(gram)
    identity = jnp.broadcast_to(jnp.eye(COLUMNS, dtype=jnp.float32), (FOLDS, COLUMNS, COLUMNS))
    inverse = jax.scipy.linalg.solve_triangular(lower_factor, identity, lower=True)
    point_scale = (inverse * jnp.float32(total**0.5)).astype(jnp.bfloat16)
    point_basis = jnp.einsum(
        "fkj,fjp->fkp", point_scale, folded, preferred_element_type=jnp.float32
    )
    point_basis = point_basis.astype(jnp.bfloat16).reshape(FOLDS * COLUMNS, point_cols)
    sample_scale = inverse * jnp.float32((SAMPLES / total) ** 0.5)
    sample_basis = jnp.einsum("fsj,fkj->fsk", cross, sample_scale, precision=lax.Precision.HIGHEST)
    return (point_basis, sample_basis)


def solution(mesh):
    in_specs = (P(None, AXES), P(AXES), P("lat", "lon"), P())
    out_specs = (P(None, AXES), P())
    return jax.shard_map(
        on_device, mesh=mesh, in_specs=in_specs, out_specs=out_specs, check_vma=False
    )
```

time: 254 us -> 146 us (0.57)
  waiting for transfers between devices: 132 us -> 28.5 us
  between operations: 14.8 us -> 1.38 us
  starting transfers between devices: 0.04 us -> 9.09 us
  matrix products: 17.5 us -> 10.4 us
  other arithmetic: 87.7 us -> 93.9 us
    psum x1 -> x0, waiting for transfers between devices: 132 us -> none  [grid_total(): return lax.psum(partial_value, ('lat', 'lon'))]
    ppermute x0 -> x5, waiting for transfers between devices: none -> 28.5 us  [grid_total(): value = value + lax.ppermute(value, AXES, pairs)]
    ppermute x0 -> x5, starting transfers between devices: none -> 9.09 us  [grid_total(): value = value + lax.ppermute(value, AXES, pairs)]
    dot_general x2 -> x3, matrix products: 9.55 us -> 4.11 us  [the longest x1 2.59 us: on_device(): jnp.einsum('sp,tp->st', weighted, weighted, preferred_element_type=jnp.fl...]
    another operation x3, other arithmetic: 39.4 us -> 42.5 us  [on_device(): jax.scipy.linalg.solve_triangular(lower_factor, identity, lower=True)]
  transfers between devices with their start and end apart: 1 -> 5, of which waited for: 1 -> 5; matrix products, arithmetic and copies ran while one was open for 0% -> 1% of each run, Pallas kernels for 0% -> 0%
where the time goes in v1:
time: 146 us; the launch traced here: 145 us
  other arithmetic  93.9 us (64%)
  waiting for transfers between devices  28.5 us (20%)
  matrix products  10.4 us (7%)
  starting transfers between devices  9.09 us (6%)
  local copies, waits for them, and re-layouts  1.8 us (1%)
    another operation x4, other arithmetic, on_device(): lower_factor = jnp.linalg.cholesky(gram)  49.4 us
    another operation x3, other arithmetic, on_device(): jax.scipy.linalg.solve_triangular(lower_factor, identity, lower=True)  42.5 us
    ppermute x5, waiting for transfers between devices, grid_total(): value = value + lax.ppermute(value, AXES, pairs)  28.5 us
    ppermute x5, starting transfers between devices, grid_total(): value = value + lax.ppermute(value, AXES, pairs)  9.09 us
  transfers between devices with their start and end apart: 5, of which 5 were waited for; matrix products, arithmetic and copies ran while one was open for 1% of the time, Pallas kernels for 0%

profile of v1, /device:TPU:0, one launch (start us, length us, event | category | flops | bytes accessed | tf_op | source)
XLA Modules:
  0.0 145.1 jit_solution(5516491181531998755)
XLA Ops:
  1.3 0.0 copy-start.1
  1.3 2.6 %fusion = f32[256,256]{1,0:T(8,128)S(1)} fusion(bf16[256,2816]{1,0:T(8,128)(2,1)} %param.4, f32[2816]{0:T(1024)} %param.5, pred[2816]{0:T(1024)(128)(4,1)S(1)} %iota_compare_fusion.2), kind=kOutput, calls=%fused_computation.3 | convolution fusion | flops 371982336 | bytes 1718016 | tf_op jit(solution)/shard_map/sp,tp->st/dot_general | solution.py:35
  3.9 0.0 copy-start
  3.9 0.0 copy-start.2
  3.9 0.5 collective-permute-start
  4.4 1.2 collective-permute-done
  5.6 2.9 %collective-permute-start.1 = (f32[256,256]{1,0:T(8,128)S(1)}, f32[256,256]{1,0:T(8,128)S(1)}, u32[]{:S(2)}, u32[]{:S(2)}) collective-permute-start(f32[256,256]{1,0:T(8,128)S(1)} %add.37), channel_id=1, source_target_pairs={{0,2},{1,3},{2,0},{3,1},{4,6},{5,7},{6,4},{7,5},{8,10},{9,11},{10,... | collective-permute-start | bytes 786440 | tf_op jit(solution)/shard_map/ppermute | solution.py:20
  8.6 6.6 %collective-permute-done.1 = f32[256,256]{1,0:T(8,128)S(1)} collective-permute-done((f32[256,256]{1,0:T(8,128)S(1)}, f32[256,256]{1,0:T(8,128)S(1)}, u32[]{:S(2)}, u32[]{:S(2)}) %collective-permute-start.1) | collective-permute-done | bytes 262176 | tf_op jit(solution)/shard_map/ppermute | solution.py:20
  15.2 1.8 %collective-permute-start.2 = (f32[256,256]{1,0:T(8,128)S(1)}, f32[256,256]{1,0:T(8,128)S(1)}, u32[]{:S(2)}, u32[]{:S(2)}) collective-permute-start(f32[256,256]{1,0:T(8,128)S(1)} %add.38), channel_id=1, source_target_pairs={{0,4},{1,5},{2,6},{3,7},{4,0},{5,1},{6,2},{7,3},{8,12},{9,13},{10,... | collective-permute-start | bytes 786440 | tf_op jit(solution)/shard_map/ppermute | solution.py:20
  17.1 6.0 %collective-permute-done.2 = f32[256,256]{1,0:T(8,128)S(1)} collective-permute-done((f32[256,256]{1,0:T(8,128)S(1)}, f32[256,256]{1,0:T(8,128)S(1)}, u32[]{:S(2)}, u32[]{:S(2)}) %collective-permute-start.2) | collective-permute-done | bytes 262176 | tf_op jit(solution)/shard_map/ppermute | solution.py:20
  23.1 1.6 %collective-permute-start.3 = (f32[256,256]{1,0:T(8,128)S(1)}, f32[256,256]{1,0:T(8,128)S(1)}, u32[]{:S(2)}, u32[]{:S(2)}) collective-permute-start(f32[256,256]{1,0:T(8,128)S(1)} %add.39), channel_id=1, source_target_pairs={{0,8},{1,9},{2,10},{3,11},{4,12},{5,13},{6,14},{7,15},{8,0},{9,1},... | collective-permute-start | bytes 786440 | tf_op jit(solution)/shard_map/ppermute | solution.py:20
  24.7 0.0 copy-done.1
  24.7 0.1 compare_select_fusion
  24.9 5.3 %collective-permute-done.3 = f32[256,256]{1,0:T(8,128)S(1)} collective-permute-done((f32[256,256]{1,0:T(8,128)S(1)}, f32[256,256]{1,0:T(8,128)S(1)}, u32[]{:S(2)}, u32[]{:S(2)}) %collective-permute-start.3) | collective-permute-done | bytes 262176 | tf_op jit(solution)/shard_map/ppermute | solution.py:20
  30.2 2.2 %collective-permute-start.4 = (f32[256,256]{1,0:T(8,128)S(1)}, f32[256,256]{1,0:T(8,128)S(1)}, u32[]{:S(2)}, u32[]{:S(2)}) collective-permute-start(f32[256,256]{1,0:T(8,128)S(1)} %add.40), channel_id=1, source_target_pairs={{0,16},{1,17},{2,18},{3,19},{4,20},{5,21},{6,22},{7,23},{8,24},{9,... | collective-permute-start | bytes 786440 | tf_op jit(solution)/shard_map/ppermute | solution.py:20
  32.4 0.0 copy-done
  32.4 0.0 copy-done.2
  32.4 0.9 convolution_convert_fusion.1
  33.4 9.4 %collective-permute-done.4 = f32[256,256]{1,0:T(8,128)S(1)} collective-permute-done((f32[256,256]{1,0:T(8,128)S(1)}, f32[256,256]{1,0:T(8,128)S(1)}, u32[]{:S(2)}, u32[]{:S(2)}) %collective-permute-start.4) | collective-permute-done | bytes 262176 | tf_op jit(solution)/shard_map/ppermute | solution.py:20
  42.8 0.4 fusion.4
  43.2 1.1 fusion.20
  44.3 1.8 %copy.8 = f32[8,64,64]{1,2,0:T(8,128)} copy(f32[8,64,64]{2,1,0:T(8,128)} %fusion.20) | data formatting | bytes 262144 | tf_op jit(solution)/shard_map/fks,fsj->fkj/dot_general | solution.py:44
  46.1 1.8 %fusion.3 = f32[8,64,64]{2,1,0:T(8,128)} fusion(f32[8,64,64]{2,1,0:T(8,128)} %fusion.20, f32[8,64,64]{1,2,0:T(8,128)} %copy.8), kind=kLoop, calls=%fused_computation.8 | loop fusion | flops 65536 | bytes 393216 | tf_op jit(solution)/shard_map/jit(cholesky)/div | solution.py:45
  47.9 48.3 %custom-call.8 = f32[8,64,64]{2,1,0:T(8,128)} custom-call(f32[8,64,64]{2,1,0:T(8,128)} %fusion.3), custom_call_target="Cholesky" | custom-call | tf_op jit(solution)/shard_map/jit(cholesky)/cholesky | solution.py:45
  96.2 1.0 select_reduce_fusion
  97.1 0.1 compare_reduce_fusion
  97.3 1.8 %select_bitcast_fusion = f32[8,1,64,64]{3,2,1,0:T(8,128)} fusion(f32[8,64,64]{2,1,0:T(8,128)} %custom-call.8, pred[8]{0:T(512)(128)(4,1)S(1)} %compare_reduce_fusion, pred[64,64]{1,0:T(8,128)(4,1)S(1)} %iota_compare_fusion.1), kind=kLoop, calls=%fused_computation.14 | loop fusion | flops 98304 | bytes 266248 | tf_op jit(solution)/shard_map/jit(_solve_triangular)/vmap()/triangular_solve | solution.py:47
  99.0 40.7 %custom-call.9 = f32[8,1,64,64]{2,3,1,0:T(8,128)} custom-call(f32[8,1,64,64]{3,2,1,0:T(8,128)} %select_bitcast_fusion), custom_call_target="InvertDiagBlocksLowerTriangular" | custom-call | tf_op jit(solution)/shard_map/jit(_solve_triangular)/vmap()/triangular_solve | solution.py:47
  139.7 1.5 %fusion.1 = f32[8,64,64]{2,1,0:T(8,128)S(1)} fusion(f32[8,1,64,64]{2,3,1,0:T(8,128)} %custom-call.9, f32[64,64]{1,0:T(8,128)S(1)} %fusion.12), kind=kOutput, calls=%fused_computation.5 | convolution fusion | flops 25165824 | bytes 278528 | tf_op jit(solution)/shard_map/jit(_solve_triangular)/vmap()/triangular_solve | solution.py:47
  141.2 1.4 fusion.6
  142.6 2.5 %convolution_convert_fusion = bf16[8,64,2816]{2,1,0:T(8,128)(2,1)} fusion(bf16[8,64,2816]{2,1,0:T(8,128)(2,1)S(1)} %bitcast.23, f32[8,64,64]{2,1,0:T(8,128)S(1)} %fusion.1), kind=kOutput, calls=%fused_computation | convolution fusion | flops 186056704 | bytes 5898240 | tf_op jit(solution)/shard_map/fkj,fjp->fkp/dot_general | solution.py:49
  (10 shorter events, 0.2 us)
Async XLA Ops:
  1.3 23.4 %copy-start.1 = (bf16[512,256]{1,0:T(8,128)(2,1)S(1)}, bf16[512,256]{1,0:T(8,128)(2,1)}, u32[]{:S(2)}) copy-start(bf16[512,256]{1,0:T(8,128)(2,1)} %param.7) | copy-start | bytes 786436
  3.9 28.5 %copy-start = (bf16[256,2816]{1,0:T(8,128)(2,1)S(1)}, bf16[256,2816]{1,0:T(8,128)(2,1)}, u32[]{:S(2)}) copy-start(bf16[256,2816]{1,0:T(8,128)(2,1)} %param.4) | copy-start | bytes 4325380
  3.9 28.5 %copy-start.2 = (f32[2816]{0:T(1024)S(1)}, f32[2816]{0:T(1024)}, u32[]{:S(2)}) copy-start(f32[2816]{0:T(1024)} %param.5) | copy-start | bytes 33796
  3.9 1.7 %collective-permute-start = (f32[256,256]{1,0:T(8,128)S(1)}, f32[256,256]{1,0:T(8,128)S(1)}, u32[]{:S(2)}, u32[]{:S(2)}) collective-permute-start(f32[256,256]{1,0:T(8,128)S(1)} %fusion), channel_id=1, source_target_pairs={{0,1},{1,0},{2,3},{3,2},{4,5},{5,4},{6,7},{7,6},{8,9},{9,8},{10,11... | collective-permute-start | bytes 786440 | tf_op jit(solution)/shard_map/ppermute | solution.py:20
  5.6 9.5 %collective-permute-start.1 = (f32[256,256]{1,0:T(8,128)S(1)}, f32[256,256]{1,0:T(8,128)S(1)}, u32[]{:S(2)}, u32[]{:S(2)}) collective-permute-start(f32[256,256]{1,0:T(8,128)S(1)} %add.37), channel_id=1, source_target_pairs={{0,2},{1,3},{2,0},{3,1},{4,6},{5,7},{6,4},{7,5},{8,10},{9,11},{10,... | collective-permute-start | bytes 786440 | tf_op jit(solution)/shard_map/ppermute | solution.py:20
  15.2 7.9 %collective-permute-start.2 = (f32[256,256]{1,0:T(8,128)S(1)}, f32[256,256]{1,0:T(8,128)S(1)}, u32[]{:S(2)}, u32[]{:S(2)}) collective-permute-start(f32[256,256]{1,0:T(8,128)S(1)} %add.38), channel_id=1, source_target_pairs={{0,4},{1,5},{2,6},{3,7},{4,0},{5,1},{6,2},{7,3},{8,12},{9,13},{10,... | collective-permute-start | bytes 786440 | tf_op jit(solution)/shard_map/ppermute | solution.py:20
  23.1 7.0 %collective-permute-start.3 = (f32[256,256]{1,0:T(8,128)S(1)}, f32[256,256]{1,0:T(8,128)S(1)}, u32[]{:S(2)}, u32[]{:S(2)}) collective-permute-start(f32[256,256]{1,0:T(8,128)S(1)} %add.39), channel_id=1, source_target_pairs={{0,8},{1,9},{2,10},{3,11},{4,12},{5,13},{6,14},{7,15},{8,0},{9,1},... | collective-permute-start | bytes 786440 | tf_op jit(solution)/shard_map/ppermute | solution.py:20
  30.2 12.6 %collective-permute-start.4 = (f32[256,256]{1,0:T(8,128)S(1)}, f32[256,256]{1,0:T(8,128)S(1)}, u32[]{:S(2)}, u32[]{:S(2)}) collective-permute-start(f32[256,256]{1,0:T(8,128)S(1)} %add.40), channel_id=1, source_target_pairs={{0,16},{1,17},{2,18},{3,19},{4,20},{5,21},{6,22},{7,23},{8,24},{9,... | collective-permute-start | bytes 786440 | tf_op jit(solution)/shard_map/ppermute | solution.py:20

commit v2 on v0

v2 whole, which is shorter than its diff:
```python
import jax
import jax.numpy as jnp
from jax import lax
from jax.experimental import pallas as pl
from jax.experimental.pallas import tpu as pltpu
from jax.sharding import PartitionSpec as P

SAMPLES = 256
COLUMNS = 64
FOLDS = 8
AXES = ("lat", "lon")
HALF = SAMPLES // 2
QUARTER = HALF // 2
PACKED = 2 * QUARTER + 8
BLOCK = 8
WIDE = 4 * COLUMNS
NT = (((1,), (1,)), ((), ()))
VMEM = pltpu.VMEM
SPLIT = 3


def iota(shape, dim):
    return lax.broadcasted_iota(jnp.int32, shape, dim)


def split_bf16(value):
    parts = []
    for _ in range(SPLIT):
        part = value.astype(jnp.bfloat16)
        parts.append(part)
        value = value - part.astype(jnp.float32)
    return parts


def dot_nt(a, b):
    return lax.dot_general(a, b, NT, preferred_element_type=jnp.float32)


def chunks_of(cols, width):
    return [(start, min(width, cols - start)) for start in range(0, cols, width)]


def cov_kernel(scalars, samples, area, weighted, mine, other, held, sems):
    cols = area.shape[1]
    parts = chunks_of(cols, 768)
    copies = []
    for n, (start, width) in enumerate(parts):
        copies.append(
            pltpu.make_async_copy(
                samples.at[:, pl.ds(start, width)], held.at[:, pl.ds(start, width)], sems.at[n]
            )
        )
        copies[-1].start()
    masked = jnp.where(iota((1, cols), 1) < scalars[0], area[...], 0.0)
    cov = jnp.zeros((SAMPLES, SAMPLES), jnp.float32)
    for copy, (start, width) in zip(copies, parts):
        copy.wait()
        part = held[:, start : start + width].astype(jnp.float32) * masked[:, start : start + width]
        part = part.astype(jnp.bfloat16)
        weighted[:, start : start + width] = part
        cov = cov + dot_nt(part, part)
    row, col = iota((HALF, HALF), 0), iota((HALF, HALF), 1)
    last = cov[HALF:, HALF:]
    diagonal = jnp.sum(jnp.where(row == col, last, 0.0), axis=0, keepdims=True)
    diagonal = jnp.broadcast_to(diagonal, (8, HALF))
    triangles = jnp.where(row >= col, cov[:HALF, :HALF], last)
    square = cov[:HALF, HALF:]
    first = scalars[1] == 0
    for ref, low in ((mine, first), (other, jnp.logical_not(first))):
        ref[:QUARTER] = jnp.where(low, triangles[:QUARTER], triangles[QUARTER:])
        ref[QUARTER:HALF] = jnp.where(low, square[:QUARTER], square[QUARTER:])
        ref[HALF:] = diagonal


def lane(value, i):
    return jnp.broadcast_to(value[:, i : i + 1], value.shape)


def eliminate(rows):
    for j in range(0, COLUMNS, BLOCK):
        pivots = [rows[j + q] for q in range(BLOCK)]
        near = range(j, min(j + 2 * BLOCK, COLUMNS))
        coef = [{i: lane(pivots[q], i) for i in near if i >= j + q} for q in range(BLOCK)]
        done = []
        for q in range(BLOCK):
            scale = lax.rsqrt(coef[q][j + q])
            done.append(pivots[q] * scale)
            for i in coef[q]:
                coef[q][i] = coef[q][i] * scale
            for r in range(q + 1, BLOCK):
                pivots[r] = pivots[r] - coef[q][j + r] * done[q]
                for i in coef[r]:
                    coef[r][i] = coef[r][i] - coef[q][j + r] * coef[q][i]
        for q in range(BLOCK):
            rows[j + q] = done[q]
        for i in range(j + BLOCK, COLUMNS):
            value = rows[i]
            for q in range(BLOCK):
                value = value - (coef[q][i] if i in coef[q] else lane(done[q], i)) * done[q]
            rows[i] = value


def finish_kernel(total, scalars, mine, other, live, scores, basis, sample_basis,
                  rows, diag, scores_v, basis_v, sample_v, sems):
    cols = scores.shape[1]
    fetch = pltpu.make_async_copy(scores, scores_v, sems.at[0])
    fetch.start()
    diag[...] = jnp.zeros_like(diag)

    first = scalars[1] == 0
    low = jnp.where(first, mine[...], other[...])
    high = jnp.where(first, other[...], mine[...])
    triangles = jnp.concatenate([low[:QUARTER], high[:QUARTER]], axis=0)
    square = jnp.concatenate([low[QUARTER:HALF], high[QUARTER:HALF]], axis=0)
    row, col = iota((HALF, HALF), 0), iota((HALF, HALF), 1)
    flipped = triangles.T
    upper = jnp.where(row >= col, triangles, flipped)
    lower = jnp.where(row < col, triangles, flipped)
    lower = jnp.where(row == col, jnp.broadcast_to(low[HALF : HALF + 1], (HALF, HALF)), lower)
    cov = jnp.concatenate(
        [
            jnp.concatenate([upper, square], axis=1),
            jnp.concatenate([square.T, lower], axis=1),
        ],
        axis=0,
    )
    cov_parts = split_bf16(cov)
    test = live[...]
    mixed = jnp.zeros((FOLDS * COLUMNS, SAMPLES), jnp.float32)
    for part in cov_parts:
        mixed = mixed + jnp.dot(test, part, preferred_element_type=jnp.float32)
    eye = (iota((COLUMNS, COLUMNS), 0) == iota((COLUMNS, COLUMNS), 1)).astype(jnp.float32)
    for f in range(FOLDS):
        own = slice(f * COLUMNS, (f + 1) * COLUMNS)
        gram = jnp.zeros((COLUMNS, COLUMNS), jnp.float32)
        for part in split_bf16(mixed[own]):
            gram = gram + dot_nt(part, test[own])
        rows[:, f, :] = jnp.concatenate([gram, eye], axis=1)

    eliminate(rows)

    in_low = iota((COLUMNS, 2 * COLUMNS), 1) < COLUMNS
    for f in range(FOLDS):
        inverse = rows[:, f, :]
        if f % 2 == 0:
            inverse = jnp.where(in_low, pltpu.roll(inverse, COLUMNS, 1), 0.0)
        else:
            inverse = jnp.where(in_low, 0.0, inverse)
        at = (f % 4) // 2 * 2 * COLUMNS
        diag[f * COLUMNS : (f + 1) * COLUMNS, at : at + 2 * COLUMNS] = inverse

    fetch.wait()
    copies = []
    for g in range(FOLDS // 4):
        own = slice(g * WIDE, (g + 1) * WIDE)
        scale = (diag[own] * jnp.float32(total**0.5)).astype(jnp.bfloat16)
        for n, (start, width) in enumerate(chunks_of(cols, 768)):
            at = slice(start, start + width)
            basis_v[own, at] = jnp.dot(
                scale, scores_v[own, at], preferred_element_type=jnp.float32
            ).astype(jnp.bfloat16)
            where = (pl.ds(g * WIDE, WIDE), pl.ds(start, width))
            copies.append(
                pltpu.make_async_copy(basis_v.at[where], basis.at[where], sems.at[1 + len(copies)])
            )
            copies[-1].start()
    for g in range(FOLDS // 4):
        own = slice(g * WIDE, (g + 1) * WIDE)
        sample_v[own] = jnp.dot(
            diag[own] * jnp.float32((SAMPLES / total) ** 0.5), mixed[own],
            precision=lax.Precision.HIGHEST, preferred_element_type=jnp.float32,
        )
        where = pl.ds(g * WIDE, WIDE)
        copies.append(
            pltpu.make_async_copy(
                sample_v.at[where], sample_basis.at[where], sems.at[1 + len(copies)]
            )
        )
        copies[-1].start()
    for copy in copies:
        copy.wait()


def spec(space):
    return pl.BlockSpec(memory_space=space)


def grid_total(mine, other):
    devices = lax.axis_size("lat") * lax.axis_size("lon")
    bits = []
    while 2 << len(bits) < devices:
        bits.append(2 << len(bits))
    assert devices == 2 << len(bits)
    near, far = bits[: len(bits) // 2], bits[len(bits) // 2 :]
    order = [bit for pair in zip(near, far) for bit in pair] + far[len(near) :]
    swap = [bit for pair in zip(far, near) for bit in pair] + far[len(near) :]
    total = mine + lax.ppermute(other, AXES, [(d, d ^ 1) for d in range(devices)])
    for bit in zip(order, swap):
        pairs = [(d, d ^ bit[d % 2]) for d in range(devices)]
        total = total + lax.ppermute(total, AXES, pairs)
    return total, lax.ppermute(total, AXES, [(d, d ^ 1) for d in range(devices)])


def on_device(samples, area_weight, ocean_count, omega):
    cols = samples.shape[1]
    total = cols * lax.axis_size("lat") * lax.axis_size("lon")
    core = lax.axis_index("lon") % 2
    scalars = jnp.stack([ocean_count[0, 0], core])
    half = jax.ShapeDtypeStruct((PACKED, HALF), jnp.float32)
    weighted, mine, other = pl.pallas_call(
        cov_kernel,
        out_shape=(jax.ShapeDtypeStruct((SAMPLES, cols), jnp.bfloat16), half, half),
        in_specs=[spec(pltpu.SMEM), spec(pl.ANY), spec(VMEM)],
        out_specs=(spec(VMEM), spec(VMEM), spec(VMEM)),
        scratch_shapes=[VMEM((SAMPLES, cols), jnp.bfloat16), pltpu.SemaphoreType.DMA((8,))],
        cost_estimate=pl.CostEstimate(
            flops=2 * SAMPLES * SAMPLES * cols, bytes_accessed=4 * SAMPLES * cols, transcendentals=0
        ),
        compiler_params=pltpu.CompilerParams(vmem_limit_bytes=16 << 20),
        name="cov",
    )(scalars, samples, area_weight.reshape(1, cols))

    mine, other = grid_total(mine, other)

    fold_row = lax.iota(jnp.int32, FOLDS * COLUMNS) // COLUMNS
    fold_col = lax.iota(jnp.int32, SAMPLES) // (SAMPLES // FOLDS)
    keeping = fold_row[:, None] != fold_col[None, :]
    live = jnp.where(keeping, omega, jnp.zeros_like(omega))
    product = jnp.dot(live, weighted, preferred_element_type=jnp.float32)
    scores = product.astype(jnp.bfloat16)

    point_basis, sample_basis = pl.pallas_call(
        lambda *refs: finish_kernel(total, *refs),
        out_shape=(
            jax.ShapeDtypeStruct((FOLDS * COLUMNS, cols), jnp.bfloat16),
            jax.ShapeDtypeStruct((FOLDS * COLUMNS, SAMPLES), jnp.float32),
        ),
        in_specs=[spec(pltpu.SMEM), spec(VMEM), spec(VMEM), spec(VMEM), spec(pl.ANY)],
        out_specs=(spec(pl.ANY), spec(pl.ANY)),
        scratch_shapes=[
            VMEM((COLUMNS, FOLDS, 2 * COLUMNS), jnp.float32),
            VMEM((FOLDS * COLUMNS, WIDE), jnp.float32),
            VMEM((FOLDS * COLUMNS, cols), jnp.bfloat16),
            VMEM((FOLDS * COLUMNS, cols), jnp.bfloat16),
            VMEM((FOLDS * COLUMNS, SAMPLES), jnp.float32),
            pltpu.SemaphoreType.DMA((16,)),
        ],
        compiler_params=pltpu.CompilerParams(vmem_limit_bytes=16 << 20),
        name="finish",
    )(scalars, mine, other, live, scores)
    sample_basis = sample_basis.reshape(FOLDS, COLUMNS, SAMPLES)
    return point_basis, sample_basis.transpose(0, 2, 1)


def solution(mesh):
    in_specs = (P(None, AXES), P(AXES), P("lat", "lon"), P())
    out_specs = (P(None, AXES), P())
    return jax.shard_map(
        on_device, mesh=mesh, in_specs=in_specs, out_specs=out_specs, check_vma=False
    )
```

time: 254 us -> 36 us (0.14)
  waiting for transfers between devices: 132 us -> 10.3 us
  other arithmetic: 87.7 us -> 0.27 us
  matrix products: 17.5 us -> 0.91 us
  between operations: 14.8 us -> 1.33 us
  starting transfers between devices: 0.04 us -> 10.8 us
  Pallas kernels: 0 us -> 10 us
    psum x1 -> x0, waiting for transfers between devices: 132 us -> none  [grid_total(): return lax.psum(partial_value, ('lat', 'lon'))]
    another operation x7 -> x1, other arithmetic: 86.7 us -> 0.07 us  [on_device(): scalars = jnp.stack([ocean_count[0, 0], core])]
    dot_general x4 -> x0, matrix products: 14.5 us -> none  [the longest x1 5.85 us: on_device(): jnp.einsum('fkp,fjp->fkj', exact, exact, precision=lax.Precision.HIGHEST)]
    ppermute x0 -> x6, starting transfers between devices: none -> 10.8 us  [the longest x4 10.2 us: grid_total(): total = total + lax.ppermute(total, AXES, pairs)]
    ppermute x0 -> x6, waiting for transfers between devices: none -> 10.3 us  [the longest x4 9.06 us: grid_total(): total = total + lax.ppermute(total, AXES, pairs)]
    pallas_call x0 -> x2, Pallas kernels: none -> 10 us  [the longest x1 8.12 us: on_device(): pl.pallas_call(lambda *refs: finish_kernel(total, *refs), out_shape=(jax....]
  transfers between devices with their start and end apart: 1 -> 6, of which waited for: 1 -> 6; matrix products, arithmetic and copies ran while one was open for 0% -> 3% of each run, Pallas kernels for 0% -> 0%
where the time goes in v2:
time: 36 us; the launch traced here: 35.7 us
  starting transfers between devices  10.8 us (30%)
  waiting for transfers between devices  10.3 us (29%)
  Pallas kernels  10 us (28%)
  local copies, waits for them, and re-layouts  2.08 us (6%)
  between operations  1.33 us (4%)
  matrix products  0.91 us (3%)
    ppermute x4, starting transfers between devices, grid_total(): total = total + lax.ppermute(total, AXES, pairs)  10.2 us
    ppermute x4, waiting for transfers between devices, grid_total(): total = total + lax.ppermute(total, AXES, pairs)  9.06 us
    pallas_call x1, Pallas kernels, on_device(): pl.pallas_call(lambda *refs: finish_kernel(total, *refs), out_shape=(jax....  8.12 us
    pallas_call x1, Pallas kernels, on_device(): pl.pallas_call(cov_kernel, out_shape=(jax.ShapeDtypeStruct((SAMPLES, cols...  1.92 us
    unnamed x4, local copies, waits for them, and re-layouts  1.37 us
    dot_general x1, matrix products, on_device(): product = jnp.dot(live, weighted, preferred_element_type=jnp.float32)  0.91 us
    ppermute x1, waiting for transfers between devices, grid_total(): lax.ppermute(other, AXES, [(d, d ^ 1) for d in range(devices)])  0.91 us
  transfers between devices with their start and end apart: 6, of which 6 were waited for; matrix products, arithmetic and copies ran while one was open for 3% of the time, Pallas kernels for 0%

profile of v2, /device:TPU:0, one launch (start us, length us, event | category | flops | bytes accessed | tf_op | source)
XLA Modules:
  0.0 35.7 jit_solution(2564753203309313158)
XLA Ops:
  1.3 0.7 %reshape.36.area = f32[1,2816]{1,0:T(1,128)S(1)} reshape(f32[2816]{0:T(1024)} %param.5) | data formatting | bytes 22528 | tf_op jit(solution)/shard_map/reshape | solution.py:221
  2.0 0.1 pad_add_fusion.scalars.refs_0_
  2.1 0.0 copy-start
  2.1 1.4 %copy-done = bf16[256,2816]{1,0:T(8,128)(2,1)S(1)} copy-done((bf16[256,2816]{1,0:T(8,128)(2,1)S(1)}, bf16[256,2816]{1,0:T(8,128)(2,1)}, u32[]{:S(2)}) %copy-start) | copy-done | bytes 1441816
  3.4 0.0 copy-start.1
  3.4 1.9 %cov.1 = (bf16[256,2816]{1,0:T(8,128)(2,1)S(1)}, f32[136,128]{1,0:T(8,128)S(1)}, f32[136,128]{1,0:T(8,128)S(1)}) custom-call(s32[2]{0:T(128)S(1)} %pad_add_fusion.scalars.refs_0_, bf16[256,2816]{1,0:T(8,128)(2,1)S(1)} %copy-done, f32[1,2816]{1,0:T(1,128)S(1)} %reshape.36.area), custom_call_target="tpu_custom_call" | custom-call | flops 369098752 | bytes 2883584 | tf_op jit(solution)/shard_map/cov/pallas_call | solution.py:210
  5.4 0.5 %collective-permute-start = (f32[136,128]{1,0:T(8,128)S(1)}, f32[136,128]{1,0:T(8,128)S(1)}, u32[]{:S(2)}, u32[]{:S(2)}) collective-permute-start(f32[136,128]{1,0:T(8,128)S(1)} %get-tuple-element.8), channel_id=1, source_target_pairs={{0,1},{1,0},{2,3},{3,2},{4,5},{5,4},{6,7},{7,6},{8,9},{9,8},{10,11... | collective-permute-start | bytes 208904 | tf_op jit(solution)/shard_map/ppermute | solution.py:197
  5.9 0.9 %collective-permute-done = f32[136,128]{1,0:T(8,128)S(1)} collective-permute-done((f32[136,128]{1,0:T(8,128)S(1)}, f32[136,128]{1,0:T(8,128)S(1)}, u32[]{:S(2)}, u32[]{:S(2)}) %collective-permute-start) | collective-permute-done | bytes 69664 | tf_op jit(solution)/shard_map/ppermute | solution.py:197
  6.8 2.9 %collective-permute-start.1 = (f32[136,128]{1,0:T(8,128)S(1)}, f32[136,128]{1,0:T(8,128)S(1)}, u32[]{:S(2)}, u32[]{:S(2)}) collective-permute-start(f32[136,128]{1,0:T(8,128)S(1)} %add.30), channel_id=1, source_target_pairs={{0,2},{1,9},{2,0},{3,11},{4,6},{5,13},{6,4},{7,15},{8,10},{9,1},{1... | collective-permute-start | bytes 208904 | tf_op jit(solution)/shard_map/ppermute | solution.py:200
  9.7 2.3 %collective-permute-done.1 = f32[136,128]{1,0:T(8,128)S(1)} collective-permute-done((f32[136,128]{1,0:T(8,128)S(1)}, f32[136,128]{1,0:T(8,128)S(1)}, u32[]{:S(2)}, u32[]{:S(2)}) %collective-permute-start.1) | collective-permute-done | bytes 69664 | tf_op jit(solution)/shard_map/ppermute | solution.py:200
  12.0 2.2 %collective-permute-start.2 = (f32[136,128]{1,0:T(8,128)S(1)}, f32[136,128]{1,0:T(8,128)S(1)}, u32[]{:S(2)}, u32[]{:S(2)}) collective-permute-start(f32[136,128]{1,0:T(8,128)S(1)} %add.31), channel_id=1, source_target_pairs={{0,8},{1,3},{2,10},{3,1},{4,12},{5,7},{6,14},{7,5},{8,0},{9,11},{1... | collective-permute-start | bytes 208904 | tf_op jit(solution)/shard_map/ppermute | solution.py:200
  14.2 2.3 %collective-permute-done.2 = f32[136,128]{1,0:T(8,128)S(1)} collective-permute-done((f32[136,128]{1,0:T(8,128)S(1)}, f32[136,128]{1,0:T(8,128)S(1)}, u32[]{:S(2)}, u32[]{:S(2)}) %collective-permute-start.2) | collective-permute-done | bytes 69664 | tf_op jit(solution)/shard_map/ppermute | solution.py:200
  16.5 2.0 %collective-permute-start.3 = (f32[136,128]{1,0:T(8,128)S(1)}, f32[136,128]{1,0:T(8,128)S(1)}, u32[]{:S(2)}, u32[]{:S(2)}) collective-permute-start(f32[136,128]{1,0:T(8,128)S(1)} %add.32), channel_id=1, source_target_pairs={{0,4},{1,17},{2,6},{3,19},{4,0},{5,21},{6,2},{7,23},{8,12},{9,25},... | collective-permute-start | bytes 208904 | tf_op jit(solution)/shard_map/ppermute | solution.py:200
  18.5 2.3 %collective-permute-done.3 = f32[136,128]{1,0:T(8,128)S(1)} collective-permute-done((f32[136,128]{1,0:T(8,128)S(1)}, f32[136,128]{1,0:T(8,128)S(1)}, u32[]{:S(2)}, u32[]{:S(2)}) %collective-permute-start.3) | collective-permute-done | bytes 69664 | tf_op jit(solution)/shard_map/ppermute | solution.py:200
  20.9 3.1 %collective-permute-start.4 = (f32[136,128]{1,0:T(8,128)S(1)}, f32[136,128]{1,0:T(8,128)S(1)}, u32[]{:S(2)}, u32[]{:S(2)}) collective-permute-start(f32[136,128]{1,0:T(8,128)S(1)} %add.33), channel_id=1, source_target_pairs={{0,16},{1,5},{2,18},{3,7},{4,20},{5,1},{6,22},{7,3},{8,24},{9,13},... | collective-permute-start | bytes 208904 | tf_op jit(solution)/shard_map/ppermute | solution.py:200
  24.0 0.0 copy-done.1
  24.0 0.1 compare_select_fusion.refs_3_
  24.1 2.1 %collective-permute-done.4 = f32[136,128]{1,0:T(8,128)S(1)} collective-permute-done((f32[136,128]{1,0:T(8,128)S(1)}, f32[136,128]{1,0:T(8,128)S(1)}, u32[]{:S(2)}, u32[]{:S(2)}) %collective-permute-start.4) | collective-permute-done | bytes 69664 | tf_op jit(solution)/shard_map/ppermute | solution.py:200
  26.3 0.1 collective-permute-start.5
  26.4 0.9 %convolution_convert_fusion.refs_4_ = bf16[512,2816]{1,0:T(8,128)(2,1)S(1)} fusion(bf16[512,256]{1,0:T(8,128)(2,1)S(1)} %compare_select_fusion.refs_3_, bf16[256,2816]{1,0:T(8,128)(2,1)S(1)} %get-tuple-element.9), kind=kOutput, calls=%fused_computation | convolution fusion | flops 739639296 | bytes 4587520 | tf_op jit(solution)/shard_map/dot_general | solution.py:229
  27.3 0.3 collective-permute-done.5.refs_2_
  27.6 8.1 %finish.1 = (bf16[512,2816]{1,0:T(8,128)(2,1)}, f32[512,256]{1,0:T(8,128)}) custom-call(s32[2]{0:T(128)S(1)} %pad_add_fusion.scalars.refs_0_, f32[136,128]{1,0:T(8,128)S(1)} %add.34.refs_1_, f32[136,128]{1,0:T(8,128)S(1)} %collective-permute-done.5.refs_2_, bf16[512,256]{1,0:T(8,128)(2,1)S(1)} %compare_select_fusion.refs_3_, ...), custom_call_target="tpu_custom_call" | custom-call | tf_op jit(solution)/shard_map/finish/pallas_call | solution.py:232
  (7 shorter events, 0.1 us)
Async XLA Ops:
  2.1 1.4 %copy-start = (bf16[256,2816]{1,0:T(8,128)(2,1)S(1)}, bf16[256,2816]{1,0:T(8,128)(2,1)}, u32[]{:S(2)}) copy-start(bf16[256,2816]{1,0:T(8,128)(2,1)} %samples.1) | copy-start | bytes 4325380
  3.4 20.5 %copy-start.1 = (bf16[512,256]{1,0:T(8,128)(2,1)S(1)}, bf16[512,256]{1,0:T(8,128)(2,1)}, u32[]{:S(2)}) copy-start(bf16[512,256]{1,0:T(8,128)(2,1)} %param.7) | copy-start | bytes 786436
  5.4 1.4 %collective-permute-start = (f32[136,128]{1,0:T(8,128)S(1)}, f32[136,128]{1,0:T(8,128)S(1)}, u32[]{:S(2)}, u32[]{:S(2)}) collective-permute-start(f32[136,128]{1,0:T(8,128)S(1)} %get-tuple-element.8), channel_id=1, source_target_pairs={{0,1},{1,0},{2,3},{3,2},{4,5},{5,4},{6,7},{7,6},{8,9},{9,8},{10,11... | collective-permute-start | bytes 208904 | tf_op jit(solution)/shard_map/ppermute | solution.py:197
  6.8 5.2 %collective-permute-start.1 = (f32[136,128]{1,0:T(8,128)S(1)}, f32[136,128]{1,0:T(8,128)S(1)}, u32[]{:S(2)}, u32[]{:S(2)}) collective-permute-start(f32[136,128]{1,0:T(8,128)S(1)} %add.30), channel_id=1, source_target_pairs={{0,2},{1,9},{2,0},{3,11},{4,6},{5,13},{6,4},{7,15},{8,10},{9,1},{1... | collective-permute-start | bytes 208904 | tf_op jit(solution)/shard_map/ppermute | solution.py:200
  12.0 4.5 %collective-permute-start.2 = (f32[136,128]{1,0:T(8,128)S(1)}, f32[136,128]{1,0:T(8,128)S(1)}, u32[]{:S(2)}, u32[]{:S(2)}) collective-permute-start(f32[136,128]{1,0:T(8,128)S(1)} %add.31), channel_id=1, source_target_pairs={{0,8},{1,3},{2,10},{3,1},{4,12},{5,7},{6,14},{7,5},{8,0},{9,11},{1... | collective-permute-start | bytes 208904 | tf_op jit(solution)/shard_map/ppermute | solution.py:200
  16.5 4.4 %collective-permute-start.3 = (f32[136,128]{1,0:T(8,128)S(1)}, f32[136,128]{1,0:T(8,128)S(1)}, u32[]{:S(2)}, u32[]{:S(2)}) collective-permute-start(f32[136,128]{1,0:T(8,128)S(1)} %add.32), channel_id=1, source_target_pairs={{0,4},{1,17},{2,6},{3,19},{4,0},{5,21},{6,2},{7,23},{8,12},{9,25},... | collective-permute-start | bytes 208904 | tf_op jit(solution)/shard_map/ppermute | solution.py:200
  20.9 5.4 %collective-permute-start.4 = (f32[136,128]{1,0:T(8,128)S(1)}, f32[136,128]{1,0:T(8,128)S(1)}, u32[]{:S(2)}, u32[]{:S(2)}) collective-permute-start(f32[136,128]{1,0:T(8,128)S(1)} %add.33), channel_id=1, source_target_pairs={{0,16},{1,5},{2,18},{3,7},{4,20},{5,1},{6,22},{7,3},{8,24},{9,13},... | collective-permute-start | bytes 208904 | tf_op jit(solution)/shard_map/ppermute | solution.py:200
  26.3 1.3 %collective-permute-start.5 = (f32[136,128]{1,0:T(8,128)S(1)}, f32[136,128]{1,0:T(8,128)S(1)}, u32[]{:S(2)}, u32[]{:S(2)}) collective-permute-start(f32[136,128]{1,0:T(8,128)S(1)} %add.34.refs_1_), channel_id=1, source_target_pairs={{0,1},{1,0},{2,3},{3,2},{4,5},{5,4},{6,7},{7,6},{8,9},{9,8},{10,11... | collective-permute-start | bytes 208904 | tf_op jit(solution)/shard_map/ppermute | solution.py:201

commit v3 on v2

--- a/solution.py
+++ b/solution.py
@@ -40,9 +40,11 @@
     return [(start, min(width, cols - start)) for start in range(0, cols, width)]
 
 
-def cov_kernel(scalars, samples, area, weighted, mine, other, held, sems):
-    cols = area.shape[1]
+def cov_kernel(count, samples, area, weighted, mine, other, held, area_v, sems):
+    cols = samples.shape[1]
     parts = chunks_of(cols, 768)
+    fetch = pltpu.make_async_copy(area, area_v.at[0], sems.at[len(parts)])
+    fetch.start()
     copies = []
     for n, (start, width) in enumerate(parts):
         copies.append(
@@ -51,7 +53,8 @@
             )
         )
         copies[-1].start()
-    masked = jnp.where(iota((1, cols), 1) < scalars[0], area[...], 0.0)
+    fetch.wait()
+    masked = jnp.where(iota((1, cols), 1) < count[0, 0], area_v[...], 0.0)
     cov = jnp.zeros((SAMPLES, SAMPLES), jnp.float32)
     for copy, (start, width) in zip(copies, parts):
         copy.wait()
@@ -65,7 +68,7 @@
     diagonal = jnp.broadcast_to(diagonal, (8, HALF))
     triangles = jnp.where(row >= col, cov[:HALF, :HALF], last)
     square = cov[:HALF, HALF:]
-    first = scalars[1] == 0
+    first = lax.axis_index("lon") % 2 == 0
     for ref, low in ((mine, first), (other, jnp.logical_not(first))):
         ref[:QUARTER] = jnp.where(low, triangles[:QUARTER], triangles[QUARTER:])
         ref[QUARTER:HALF] = jnp.where(low, square[:QUARTER], square[QUARTER:])
@@ -76,38 +79,59 @@
     return jnp.broadcast_to(value[:, i : i + 1], value.shape)
 
 
+def take(value, index):
+    return jnp.take_along_axis(value, index, axis=1, mode="promise_in_bounds")
+
+
 def eliminate(rows):
+    at = iota((FOLDS, 2 * COLUMNS), 1)
+    even = at < COLUMNS
+    column = jnp.where(even, at, at - COLUMNS)
+    odd = jnp.where(even, 0, 1)
     for j in range(0, COLUMNS, BLOCK):
-        pivots = [rows[j + q] for q in range(BLOCK)]
-        near = range(j, min(j + 2 * BLOCK, COLUMNS))
-        coef = [{i: lane(pivots[q], i) for i in near if i >= j + q} for q in range(BLOCK)]
+        raw = []
+        for p in range(j // 2, (j + BLOCK) // 2):
+            pair = rows[p]
+            swapped = pltpu.roll(pair, COLUMNS, 1)
+            raw += [jnp.where(even, pair, swapped), jnp.where(even, swapped, pair)]
+        near = range((j + BLOCK) // 2, min(j // 2 + BLOCK, COLUMNS // 2))
+        coef = [{r: lane(raw[q], j + r) for r in range(q, BLOCK)} for q in range(BLOCK)]
+        pairs = [{p: take(raw[q], odd + 2 * p) for p in near} for q in range(BLOCK)]
+        inside = (column >= j) & (column < j + BLOCK)
+        pivots = [jnp.where(inside, 0.0, value) for value in raw]
         done = []
         for q in range(BLOCK):
-            scale = lax.rsqrt(coef[q][j + q])
-            done.append(pivots[q] * scale)
-            for i in coef[q]:
-                coef[q][i] = coef[q][i] * scale
+            scale = lax.rsqrt(coef[q][q])
+            done.append(jnp.where(column == j + q, scale, pivots[q] * scale))
+            for have in (coef[q], pairs[q]):
+                for i in have:
+                    have[i] = have[i] * scale
             for r in range(q + 1, BLOCK):
-                pivots[r] = pivots[r] - coef[q][j + r] * done[q]
-                for i in coef[r]:
-                    coef[r][i] = coef[r][i] - coef[q][j + r] * coef[q][i]
-        for q in range(BLOCK):
-            rows[j + q] = done[q]
-        for i in range(j + BLOCK, COLUMNS):
-            value = rows[i]
+                factor = coef[q][r]
+                pivots[r] = pivots[r] - factor * done[q]
+                for have, used in ((coef, coef[r]), (pairs, pairs[r])):
+                    for i in used:
+                        used[i] = used[i] - factor * have[q][i]
+        for q in range(0, BLOCK, 2):
+            rows[(j + q) // 2] = jnp.where(even, done[q], done[q + 1])
+        for p in range((j + BLOCK) // 2, COLUMNS // 2):
+            value = jnp.where(inside, 0.0, rows[p])
             for q in range(BLOCK):
-                value = value - (coef[q][i] if i in coef[q] else lane(done[q], i)) * done[q]
-            rows[i] = value
-
-
-def finish_kernel(total, scalars, mine, other, live, scores, basis, sample_basis,
-                  rows, diag, scores_v, basis_v, sample_v, sems):
+                factor = pairs[q][p] if p in near else take(done[q], odd + 2 * p)
+                value = value - factor * done[q]
+            rows[p] = value
+
+
+def beside(ref, rows):
+    return jnp.concatenate([ref[0, rows, :], ref[1, rows, :]], axis=1)
+
+
+def finish_kernel(total, mine, other, live, scores, basis, sample_basis,
+                  rows, diag, mixed_v, basis_v, sample_v, sems):
     cols = scores.shape[1]
-    fetch = pltpu.make_async_copy(scores, scores_v, sems.at[0])
-    fetch.start()
     diag[...] = jnp.zeros_like(diag)
 
-    first = scalars[1] == 0
+    first = lax.axis_index("lon") % 2 == 0
     low = jnp.where(first, mine[...], other[...])
     high = jnp.where(first, other[...], mine[...])
     triangles = jnp.concatenate([low[:QUARTER], high[:QUARTER]], axis=0)
@@ -129,51 +153,56 @@
     mixed = jnp.zeros((FOLDS * COLUMNS, SAMPLES), jnp.float32)
     for part in cov_parts:
         mixed = mixed + jnp.dot(test, part, preferred_element_type=jnp.float32)
-    eye = (iota((COLUMNS, COLUMNS), 0) == iota((COLUMNS, COLUMNS), 1)).astype(jnp.float32)
+    for c in (0, 1):
+        mixed_v[c] = mixed[:, c * HALF : (c + 1) * HALF]
+    pairs = COLUMNS // 2
     for f in range(FOLDS):
-        own = slice(f * COLUMNS, (f + 1) * COLUMNS)
+        even, odd = (
+            beside(mixed_v, pl.ds(f * COLUMNS + o, pairs, stride=2)) for o in (0, 1)
+        )
+        own = test[f * COLUMNS : (f + 1) * COLUMNS]
         gram = jnp.zeros((COLUMNS, COLUMNS), jnp.float32)
-        for part in split_bf16(mixed[own]):
-            gram = gram + dot_nt(part, test[own])
-        rows[:, f, :] = jnp.concatenate([gram, eye], axis=1)
+        for part in split_bf16(jnp.concatenate([even, odd], axis=0)):
+            gram = gram + dot_nt(part, own)
+        rows[:, f, :] = jnp.concatenate([gram[:pairs], gram[pairs:]], axis=1)
 
     eliminate(rows)
 
-    in_low = iota((COLUMNS, 2 * COLUMNS), 1) < COLUMNS
+    at, pair = iota((pairs, 2 * COLUMNS), 1), iota((pairs, 2 * COLUMNS), 0)
     for f in range(FOLDS):
-        inverse = rows[:, f, :]
-        if f % 2 == 0:
-            inverse = jnp.where(in_low, pltpu.roll(inverse, COLUMNS, 1), 0.0)
-        else:
-            inverse = jnp.where(in_low, 0.0, inverse)
-        at = (f % 4) // 2 * 2 * COLUMNS
-        diag[f * COLUMNS : (f + 1) * COLUMNS, at : at + 2 * COLUMNS] = inverse
-
-    fetch.wait()
+        left = f % 2 == 0
+        found = rows[:, f, :]
+        swapped = pltpu.roll(found, COLUMNS, 1)
+        column = at if left else at - COLUMNS
+        for o in (0, 1):
+            keep = (column >= 0) & (column <= 2 * pair + o)
+            value = jnp.where(keep, found if left == (o == 0) else swapped, 0.0)
+            diag[f % 4 // 2, pl.ds(f * COLUMNS + o, pairs, stride=2), :] = value
+
     copies = []
     for g in range(FOLDS // 4):
         own = slice(g * WIDE, (g + 1) * WIDE)
-        scale = (diag[own] * jnp.float32(total**0.5)).astype(jnp.bfloat16)
+        scale = (beside(diag, own) * jnp.float32(total**0.5)).astype(jnp.bfloat16)
         for n, (start, width) in enumerate(chunks_of(cols, 768)):
             at = slice(start, start + width)
             basis_v[own, at] = jnp.dot(
-                scale, scores_v[own, at], preferred_element_type=jnp.float32
+                scale, scores[own, at], preferred_element_type=jnp.float32
             ).astype(jnp.bfloat16)
             where = (pl.ds(g * WIDE, WIDE), pl.ds(start, width))
             copies.append(
-                pltpu.make_async_copy(basis_v.at[where], basis.at[where], sems.at[1 + len(copies)])
+                pltpu.make_async_copy(basis_v.at[where], basis.at[where], sems.at[len(copies)])
             )
             copies[-1].start()
     for g in range(FOLDS // 4):
         own = slice(g * WIDE, (g + 1) * WIDE)
         sample_v[own] = jnp.dot(
-            diag[own] * jnp.float32((SAMPLES / total) ** 0.5), mixed[own],
+            beside(diag, own) * jnp.float32((SAMPLES / total) ** 0.5), beside(mixed_v, own),
             precision=lax.Precision.HIGHEST, preferred_element_type=jnp.float32,
         )
         where = pl.ds(g * WIDE, WIDE)
         copies.append(
             pltpu.make_async_copy(
-                sample_v.at[where], sample_basis.at[where], sems.at[1 + len(copies)]
+                sample_v.at[where], sample_basis.at[where], sems.at[len(copies)]
             )
         )
         copies[-1].start()
@@ -204,21 +233,27 @@
 def on_device(samples, area_weight, ocean_count, omega):
     cols = samples.shape[1]
     total = cols * lax.axis_size("lat") * lax.axis_size("lon")
-    core = lax.axis_index("lon") % 2
-    scalars = jnp.stack([ocean_count[0, 0], core])
     half = jax.ShapeDtypeStruct((PACKED, HALF), jnp.float32)
     weighted, mine, other = pl.pallas_call(
         cov_kernel,
         out_shape=(jax.ShapeDtypeStruct((SAMPLES, cols), jnp.bfloat16), half, half),
-        in_specs=[spec(pltpu.SMEM), spec(pl.ANY), spec(VMEM)],
+        in_specs=[spec(pltpu.SMEM), spec(pltpu.HBM), spec(pltpu.HBM)],
         out_specs=(spec(VMEM), spec(VMEM), spec(VMEM)),
-        scratch_shapes=[VMEM((SAMPLES, cols), jnp.bfloat16), pltpu.SemaphoreType.DMA((8,))],
+        scratch_shapes=[
+            VMEM((SAMPLES, cols), jnp.bfloat16),
+            VMEM((1, cols), jnp.float32),
+            pltpu.SemaphoreType.DMA((8,)),
+        ],
         cost_estimate=pl.CostEstimate(
             flops=2 * SAMPLES * SAMPLES * cols, bytes_accessed=4 * SAMPLES * cols, transcendentals=0
         ),
         compiler_params=pltpu.CompilerParams(vmem_limit_bytes=16 << 20),
         name="cov",
-    )(scalars, samples, area_weight.reshape(1, cols))
+    )(
+        ocean_count,
+        pltpu.with_memory_space_constraint(samples, pltpu.HBM),
+        pltpu.with_memory_space_constraint(area_weight, pltpu.HBM),
+    )
 
     mine, other = grid_total(mine, other)
 
@@ -235,19 +270,19 @@
             jax.ShapeDtypeStruct((FOLDS * COLUMNS, cols), jnp.bfloat16),
             jax.ShapeDtypeStruct((FOLDS * COLUMNS, SAMPLES), jnp.float32),
         ),
-        in_specs=[spec(pltpu.SMEM), spec(VMEM), spec(VMEM), spec(VMEM), spec(pl.ANY)],
+        in_specs=[spec(VMEM)] * 4,
         out_specs=(spec(pl.ANY), spec(pl.ANY)),
         scratch_shapes=[
-            VMEM((COLUMNS, FOLDS, 2 * COLUMNS), jnp.float32),
-            VMEM((FOLDS * COLUMNS, WIDE), jnp.float32),
-            VMEM((FOLDS * COLUMNS, cols), jnp.bfloat16),
+            VMEM((COLUMNS // 2, FOLDS, 2 * COLUMNS), jnp.float32),
+            VMEM((2, FOLDS * COLUMNS, WIDE // 2), jnp.float32),
+            VMEM((2, FOLDS * COLUMNS, HALF), jnp.float32),
             VMEM((FOLDS * COLUMNS, cols), jnp.bfloat16),
             VMEM((FOLDS * COLUMNS, SAMPLES), jnp.float32),
             pltpu.SemaphoreType.DMA((16,)),
         ],
         compiler_params=pltpu.CompilerParams(vmem_limit_bytes=16 << 20),
         name="finish",
-    )(scalars, mine, other, live, scores)
+    )(mine, other, live, scores)
     sample_basis = sample_basis.reshape(FOLDS, COLUMNS, SAMPLES)
     return point_basis, sample_basis.transpose(0, 2, 1)
 

time: 36 us -> 32.8 us (0.911)
  local copies, waits for them, and re-layouts: 2.08 us -> 0.01 us
  Pallas kernels: 10 us -> 8.99 us
    pallas_call x1, Pallas kernels: 8.12 us -> 6.67 us  [on_device(): pl.pallas_call(lambda *refs: finish_kernel(total, *refs), out_shape=(jax....]
    unnamed x4 -> x2, local copies, waits for them, and re-layouts: 1.37 us -> 0.01 us
    reshape x1 -> x0, local copies, waits for them, and re-layouts: 0.72 us -> none  [on_device(): area_weight.reshape(1, cols)]
    pallas_call x1, Pallas kernels: 1.92 us -> 2.32 us  [on_device(): pl.pallas_call(cov_kernel, out_shape=(jax.ShapeDtypeStruct((SAMPLES, cols...]
where the time goes in v3:
time: 32.8 us; the launch traced here: 32.6 us
  starting transfers between devices  10.8 us (33%)
  waiting for transfers between devices  10.3 us (31%)
  Pallas kernels  8.99 us (27%)
  between operations  1.38 us (4%)
  matrix products  0.91 us (3%)
    ppermute x4, starting transfers between devices, grid_total(): total = total + lax.ppermute(total, AXES, pairs)  10.2 us
    ppermute x4, waiting for transfers between devices, grid_total(): total = total + lax.ppermute(total, AXES, pairs)  9.06 us
    pallas_call x1, Pallas kernels, on_device(): pl.pallas_call(lambda *refs: finish_kernel(total, *refs), out_shape=(jax....  6.67 us
    pallas_call x1, Pallas kernels, on_device(): pl.pallas_call(cov_kernel, out_shape=(jax.ShapeDtypeStruct((SAMPLES, cols...  2.32 us
    dot_general x1, matrix products, on_device(): product = jnp.dot(live, weighted, preferred_element_type=jnp.float32)  0.91 us
    ppermute x1, waiting for transfers between devices, grid_total(): lax.ppermute(other, AXES, [(d, d ^ 1) for d in range(devices)])  0.91 us
  transfers between devices with their start and end apart: 6, of which 6 were waited for; matrix products, arithmetic and copies ran while one was open for 3% of the time, Pallas kernels for 0%

profile of v3, /device:TPU:0, one launch (start us, length us, event | category | flops | bytes accessed | tf_op | source)
XLA Modules:
  0.0 32.6 jit_solution(11615639574000356733)
XLA Ops:
  0.6 0.0 copy-start
  1.3 2.3 %cov.1 = (bf16[256,2816]{1,0:T(8,128)(2,1)S(1)}, f32[136,128]{1,0:T(8,128)S(1)}, f32[136,128]{1,0:T(8,128)S(1)}) custom-call(s32[1,1]{1,0:T(1,128)S(6)} %copy.6.count, bf16[256,2816]{1,0:T(8,128)(2,1)} %samples.1, f32[2816]{0:T(1024)} %area.1), custom_call_target="tpu_custom_call" | custom-call | flops 369098752 | bytes 2883584 | tf_op jit(solution)/shard_map/cov/pallas_call | solution.py:237
  3.7 0.5 %collective-permute-start = (f32[136,128]{1,0:T(8,128)S(1)}, f32[136,128]{1,0:T(8,128)S(1)}, u32[]{:S(2)}, u32[]{:S(2)}) collective-permute-start(f32[136,128]{1,0:T(8,128)S(1)} %get-tuple-element.8), channel_id=1, source_target_pairs={{0,1},{1,0},{2,3},{3,2},{4,5},{5,4},{6,7},{7,6},{8,9},{9,8},{10,11... | collective-permute-start | bytes 208904 | tf_op jit(solution)/shard_map/ppermute | solution.py:226
  4.2 0.9 %collective-permute-done = f32[136,128]{1,0:T(8,128)S(1)} collective-permute-done((f32[136,128]{1,0:T(8,128)S(1)}, f32[136,128]{1,0:T(8,128)S(1)}, u32[]{:S(2)}, u32[]{:S(2)}) %collective-permute-start) | collective-permute-done | bytes 69664 | tf_op jit(solution)/shard_map/ppermute | solution.py:226
  5.1 2.9 %collective-permute-start.1 = (f32[136,128]{1,0:T(8,128)S(1)}, f32[136,128]{1,0:T(8,128)S(1)}, u32[]{:S(2)}, u32[]{:S(2)}) collective-permute-start(f32[136,128]{1,0:T(8,128)S(1)} %add.25), channel_id=1, source_target_pairs={{0,2},{1,9},{2,0},{3,11},{4,6},{5,13},{6,4},{7,15},{8,10},{9,1},{1... | collective-permute-start | bytes 208904 | tf_op jit(solution)/shard_map/ppermute | solution.py:229
  8.0 2.3 %collective-permute-done.1 = f32[136,128]{1,0:T(8,128)S(1)} collective-permute-done((f32[136,128]{1,0:T(8,128)S(1)}, f32[136,128]{1,0:T(8,128)S(1)}, u32[]{:S(2)}, u32[]{:S(2)}) %collective-permute-start.1) | collective-permute-done | bytes 69664 | tf_op jit(solution)/shard_map/ppermute | solution.py:229
  10.3 2.2 %collective-permute-start.2 = (f32[136,128]{1,0:T(8,128)S(1)}, f32[136,128]{1,0:T(8,128)S(1)}, u32[]{:S(2)}, u32[]{:S(2)}) collective-permute-start(f32[136,128]{1,0:T(8,128)S(1)} %add.26), channel_id=1, source_target_pairs={{0,8},{1,3},{2,10},{3,1},{4,12},{5,7},{6,14},{7,5},{8,0},{9,11},{1... | collective-permute-start | bytes 208904 | tf_op jit(solution)/shard_map/ppermute | solution.py:229
  12.5 2.3 %collective-permute-done.2 = f32[136,128]{1,0:T(8,128)S(1)} collective-permute-done((f32[136,128]{1,0:T(8,128)S(1)}, f32[136,128]{1,0:T(8,128)S(1)}, u32[]{:S(2)}, u32[]{:S(2)}) %collective-permute-start.2) | collective-permute-done | bytes 69664 | tf_op jit(solution)/shard_map/ppermute | solution.py:229
  14.8 2.0 %collective-permute-start.3 = (f32[136,128]{1,0:T(8,128)S(1)}, f32[136,128]{1,0:T(8,128)S(1)}, u32[]{:S(2)}, u32[]{:S(2)}) collective-permute-start(f32[136,128]{1,0:T(8,128)S(1)} %add.27), channel_id=1, source_target_pairs={{0,4},{1,17},{2,6},{3,19},{4,0},{5,21},{6,2},{7,23},{8,12},{9,25},... | collective-permute-start | bytes 208904 | tf_op jit(solution)/shard_map/ppermute | solution.py:229
  16.8 2.3 %collective-permute-done.3 = f32[136,128]{1,0:T(8,128)S(1)} collective-permute-done((f32[136,128]{1,0:T(8,128)S(1)}, f32[136,128]{1,0:T(8,128)S(1)}, u32[]{:S(2)}, u32[]{:S(2)}) %collective-permute-start.3) | collective-permute-done | bytes 69664 | tf_op jit(solution)/shard_map/ppermute | solution.py:229
  19.2 3.1 %collective-permute-start.4 = (f32[136,128]{1,0:T(8,128)S(1)}, f32[136,128]{1,0:T(8,128)S(1)}, u32[]{:S(2)}, u32[]{:S(2)}) collective-permute-start(f32[136,128]{1,0:T(8,128)S(1)} %add.28), channel_id=1, source_target_pairs={{0,16},{1,5},{2,18},{3,7},{4,20},{5,1},{6,22},{7,3},{8,24},{9,13},... | collective-permute-start | bytes 208904 | tf_op jit(solution)/shard_map/ppermute | solution.py:229
  22.3 0.0 copy-done
  22.3 0.1 compare_select_fusion.refs_2_
  22.4 2.1 %collective-permute-done.4 = f32[136,128]{1,0:T(8,128)S(1)} collective-permute-done((f32[136,128]{1,0:T(8,128)S(1)}, f32[136,128]{1,0:T(8,128)S(1)}, u32[]{:S(2)}, u32[]{:S(2)}) %collective-permute-start.4) | collective-permute-done | bytes 69664 | tf_op jit(solution)/shard_map/ppermute | solution.py:229
  24.6 0.1 collective-permute-start.5
  24.6 0.9 %convolution_convert_fusion.refs_3_ = bf16[512,2816]{1,0:T(8,128)(2,1)S(1)} fusion(bf16[512,256]{1,0:T(8,128)(2,1)S(1)} %compare_select_fusion.refs_2_, bf16[256,2816]{1,0:T(8,128)(2,1)S(1)} %get-tuple-element.9), kind=kOutput, calls=%fused_computation | convolution fusion | flops 739639296 | bytes 4587520 | tf_op jit(solution)/shard_map/dot_general | solution.py:264
  25.6 0.3 %collective-permute-done.5.refs_1_ = f32[136,128]{1,0:T(8,128)S(1)} collective-permute-done((f32[136,128]{1,0:T(8,128)S(1)}, f32[136,128]{1,0:T(8,128)S(1)}, u32[]{:S(2)}, u32[]{:S(2)}) %collective-permute-start.5) | collective-permute-done | bytes 69664 | tf_op jit(solution)/shard_map/ppermute | solution.py:230
  25.9 6.7 %finish.1 = (bf16[512,2816]{1,0:T(8,128)(2,1)}, f32[512,256]{1,0:T(8,128)}) custom-call(f32[136,128]{1,0:T(8,128)S(1)} %add.29.refs_0_, f32[136,128]{1,0:T(8,128)S(1)} %collective-permute-done.5.refs_1_, bf16[512,256]{1,0:T(8,128)(2,1)S(1)} %compare_select_fusion.refs_2_, bf16[512,2816]{1,0:T(8,128)(2,1)S(1)} %convolution_convert_fusion.refs_3_), custom_call_target="tpu_custom_call" | custom-call | tf_op jit(solution)/shard_map/finish/pallas_call | solution.py:267
  (7 shorter events, 0.1 us)
Async XLA Ops:
  0.6 21.6 %copy-start = (bf16[512,256]{1,0:T(8,128)(2,1)S(1)}, bf16[512,256]{1,0:T(8,128)(2,1)}, u32[]{:S(2)}) copy-start(bf16[512,256]{1,0:T(8,128)(2,1)} %param.7) | copy-start | bytes 786436
  3.7 1.4 %collective-permute-start = (f32[136,128]{1,0:T(8,128)S(1)}, f32[136,128]{1,0:T(8,128)S(1)}, u32[]{:S(2)}, u32[]{:S(2)}) collective-permute-start(f32[136,128]{1,0:T(8,128)S(1)} %get-tuple-element.8), channel_id=1, source_target_pairs={{0,1},{1,0},{2,3},{3,2},{4,5},{5,4},{6,7},{7,6},{8,9},{9,8},{10,11... | collective-permute-start | bytes 208904 | tf_op jit(solution)/shard_map/ppermute | solution.py:226
  5.1 5.2 %collective-permute-start.1 = (f32[136,128]{1,0:T(8,128)S(1)}, f32[136,128]{1,0:T(8,128)S(1)}, u32[]{:S(2)}, u32[]{:S(2)}) collective-permute-start(f32[136,128]{1,0:T(8,128)S(1)} %add.25), channel_id=1, source_target_pairs={{0,2},{1,9},{2,0},{3,11},{4,6},{5,13},{6,4},{7,15},{8,10},{9,1},{1... | collective-permute-start | bytes 208904 | tf_op jit(solution)/shard_map/ppermute | solution.py:229
  10.3 4.5 %collective-permute-start.2 = (f32[136,128]{1,0:T(8,128)S(1)}, f32[136,128]{1,0:T(8,128)S(1)}, u32[]{:S(2)}, u32[]{:S(2)}) collective-permute-start(f32[136,128]{1,0:T(8,128)S(1)} %add.26), channel_id=1, source_target_pairs={{0,8},{1,3},{2,10},{3,1},{4,12},{5,7},{6,14},{7,5},{8,0},{9,11},{1... | collective-permute-start | bytes 208904 | tf_op jit(solution)/shard_map/ppermute | solution.py:229
  14.8 4.4 %collective-permute-start.3 = (f32[136,128]{1,0:T(8,128)S(1)}, f32[136,128]{1,0:T(8,128)S(1)}, u32[]{:S(2)}, u32[]{:S(2)}) collective-permute-start(f32[136,128]{1,0:T(8,128)S(1)} %add.27), channel_id=1, source_target_pairs={{0,4},{1,17},{2,6},{3,19},{4,0},{5,21},{6,2},{7,23},{8,12},{9,25},... | collective-permute-start | bytes 208904 | tf_op jit(solution)/shard_map/ppermute | solution.py:229
  19.2 5.4 %collective-permute-start.4 = (f32[136,128]{1,0:T(8,128)S(1)}, f32[136,128]{1,0:T(8,128)S(1)}, u32[]{:S(2)}, u32[]{:S(2)}) collective-permute-start(f32[136,128]{1,0:T(8,128)S(1)} %add.28), channel_id=1, source_target_pairs={{0,16},{1,5},{2,18},{3,7},{4,20},{5,1},{6,22},{7,3},{8,24},{9,13},... | collective-permute-start | bytes 208904 | tf_op jit(solution)/shard_map/ppermute | solution.py:229
  24.6 1.3 %collective-permute-start.5 = (f32[136,128]{1,0:T(8,128)S(1)}, f32[136,128]{1,0:T(8,128)S(1)}, u32[]{:S(2)}, u32[]{:S(2)}) collective-permute-start(f32[136,128]{1,0:T(8,128)S(1)} %add.29.refs_0_), channel_id=1, source_target_pairs={{0,1},{1,0},{2,3},{3,2},{4,5},{5,4},{6,7},{7,6},{8,9},{9,8},{10,11... | collective-permute-start | bytes 208904 | tf_op jit(solution)/shard_map/ppermute | solution.py:230

commit v4 on v3

--- a/solution.py
+++ b/solution.py
@@ -42,7 +42,7 @@
 
 def cov_kernel(count, samples, area, weighted, mine, other, held, area_v, sems):
     cols = samples.shape[1]
-    parts = chunks_of(cols, 768)
+    parts = chunks_of(cols, 1408)
     fetch = pltpu.make_async_copy(area, area_v.at[0], sems.at[len(parts)])
     fetch.start()
     copies = []
@@ -156,15 +156,32 @@
     for c in (0, 1):
         mixed_v[c] = mixed[:, c * HALF : (c + 1) * HALF]
     pairs = COLUMNS // 2
-    for f in range(FOLDS):
-        even, odd = (
-            beside(mixed_v, pl.ds(f * COLUMNS + o, pairs, stride=2)) for o in (0, 1)
+    low = iota((pairs, 2 * COLUMNS), 1) < COLUMNS
+    for g in range(FOLDS // 4):
+        folds = range(4 * g, 4 * g + 4)
+        sorted_rows = jnp.concatenate(
+            [
+                beside(mixed_v, pl.ds(f * COLUMNS + o, pairs, stride=2))
+                for f in folds
+                for o in (0, 1)
+            ],
+            axis=0,
         )
-        own = test[f * COLUMNS : (f + 1) * COLUMNS]
-        gram = jnp.zeros((COLUMNS, COLUMNS), jnp.float32)
-        for part in split_bf16(jnp.concatenate([even, odd], axis=0)):
-            gram = gram + dot_nt(part, own)
-        rows[:, f, :] = jnp.concatenate([gram[:pairs], gram[pairs:]], axis=1)
+        gram = jnp.zeros((WIDE, WIDE), jnp.float32)
+        for part in split_bf16(sorted_rows):
+            gram = gram + dot_nt(part, test[g * WIDE : (g + 1) * WIDE])
+        for f in folds:
+            at = f % 4 * COLUMNS
+            start = f % 4 // 2 * 2 * COLUMNS
+            even, odd = (
+                gram[at + o * pairs : at + (o + 1) * pairs, start : start + 2 * COLUMNS]
+                for o in (0, 1)
+            )
+            if f % 2 == 0:
+                odd = pltpu.roll(odd, COLUMNS, 1)
+            else:
+                even = pltpu.roll(even, COLUMNS, 1)
+            rows[:, f, :] = jnp.where(low, even, odd)
 
     eliminate(rows)
 
@@ -180,32 +197,28 @@
             diag[f % 4 // 2, pl.ds(f * COLUMNS + o, pairs, stride=2), :] = value
 
     copies = []
+
+    def send(source, target, where):
+        copies.append(
+            pltpu.make_async_copy(source.at[where], target.at[where], sems.at[len(copies)])
+        )
+        copies[-1].start()
+
     for g in range(FOLDS // 4):
         own = slice(g * WIDE, (g + 1) * WIDE)
-        scale = (beside(diag, own) * jnp.float32(total**0.5)).astype(jnp.bfloat16)
-        for n, (start, width) in enumerate(chunks_of(cols, 768)):
+        inverse = beside(diag, own)
+        scale = (inverse * jnp.float32(total**0.5)).astype(jnp.bfloat16)
+        for start, width in chunks_of(cols, 768):
             at = slice(start, start + width)
             basis_v[own, at] = jnp.dot(
                 scale, scores[own, at], preferred_element_type=jnp.float32
             ).astype(jnp.bfloat16)
-            where = (pl.ds(g * WIDE, WIDE), pl.ds(start, width))
-            copies.append(
-                pltpu.make_async_copy(basis_v.at[where], basis.at[where], sems.at[len(copies)])
-            )
-            copies[-1].start()
-    for g in range(FOLDS // 4):
-        own = slice(g * WIDE, (g + 1) * WIDE)
+            send(basis_v, basis, (pl.ds(g * WIDE, WIDE), pl.ds(start, width)))
         sample_v[own] = jnp.dot(
-            beside(diag, own) * jnp.float32((SAMPLES / total) ** 0.5), beside(mixed_v, own),
+            inverse * jnp.float32((SAMPLES / total) ** 0.5), beside(mixed_v, own),
             precision=lax.Precision.HIGHEST, preferred_element_type=jnp.float32,
         )
-        where = pl.ds(g * WIDE, WIDE)
-        copies.append(
-            pltpu.make_async_copy(
-                sample_v.at[where], sample_basis.at[where], sems.at[len(copies)]
-            )
-        )
-        copies[-1].start()
+        send(sample_v, sample_basis, (pl.ds(g * WIDE, WIDE),))
     for copy in copies:
         copy.wait()
 
@@ -220,14 +233,22 @@
     while 2 << len(bits) < devices:
         bits.append(2 << len(bits))
     assert devices == 2 << len(bits)
-    near, far = bits[: len(bits) // 2], bits[len(bits) // 2 :]
-    order = [bit for pair in zip(near, far) for bit in pair] + far[len(near) :]
-    swap = [bit for pair in zip(far, near) for bit in pair] + far[len(near) :]
-    total = mine + lax.ppermute(other, AXES, [(d, d ^ 1) for d in range(devices)])
-    for bit in zip(order, swap):
-        pairs = [(d, d ^ bit[d % 2]) for d in range(devices)]
-        total = total + lax.ppermute(total, AXES, pairs)
-    return total, lax.ppermute(total, AXES, [(d, d ^ 1) for d in range(devices)])
+    steps = [bits[n : n + 2] for n in range(0, len(bits), 2)]
+    turn = len(steps) // 2 if len(bits) % 2 == 0 else 0
+
+    def swap(value, even, odd):
+        pairs = [(d, d ^ (odd if d % 2 else even)) for d in range(devices)]
+        return lax.ppermute(value, AXES, pairs)
+
+    total = mine + swap(other, 1, 1)
+    for even, odd in zip(steps, steps[turn:] + steps[:turn]):
+        got = [swap(total, *bit) for bit in zip(even, odd)]
+        if len(got) == 2:
+            last = swap(total, even[0] ^ even[1], odd[0] ^ odd[1])
+            total = (total + got[0]) + (got[1] + last)
+        else:
+            total = total + got[0]
+    return total, swap(total, 1, 1)
 
 
 def on_device(samples, area_weight, ocean_count, omega):

time: 32.8 us -> 30.6 us (0.933)
  starting transfers between devices: 10.8 us -> 9.55 us
  waiting for transfers between devices: 10.3 us -> 9.68 us
  Pallas kernels: 8.99 us -> 8.64 us
    ppermute x6 -> x8, starting transfers between devices: 10.8 us -> 9.55 us  [swap(): return lax.ppermute(value, AXES, pairs)]
    ppermute x6 -> x8, waiting for transfers between devices: 10.3 us -> 9.68 us  [swap(): return lax.ppermute(value, AXES, pairs)]
  transfers between devices with their start and end apart: 6 -> 8, of which waited for: 6 -> 7; matrix products, arithmetic and copies ran while one was open for 3% -> 3% of each run, Pallas kernels for 0% -> 0%
where the time goes in v4:
time: 30.6 us; the launch traced here: 30.3 us
  waiting for transfers between devices  9.68 us (32%)
  starting transfers between devices  9.55 us (31%)
  Pallas kernels  8.64 us (28%)
  between operations  1.37 us (4%)
  matrix products  0.91 us (3%)
    ppermute x8, waiting for transfers between devices, swap(): return lax.ppermute(value, AXES, pairs)  9.68 us
    ppermute x8, starting transfers between devices, swap(): return lax.ppermute(value, AXES, pairs)  9.55 us
    pallas_call x1, Pallas kernels, on_device(): pl.pallas_call(lambda *refs: finish_kernel(total, *refs), out_shape=(jax....  6.63 us
    pallas_call x1, Pallas kernels, on_device(): pl.pallas_call(cov_kernel, out_shape=(jax.ShapeDtypeStruct((SAMPLES, cols...  2.01 us
    dot_general x1, matrix products, on_device(): product = jnp.dot(live, weighted, preferred_element_type=jnp.float32)  0.91 us
  transfers between devices with their start and end apart: 8, of which 7 were waited for; matrix products, arithmetic and copies ran while one was open for 3% of the time, Pallas kernels for 0%

profile of v4, /device:TPU:0, one launch (start us, length us, event | category | flops | bytes accessed | tf_op | source)
XLA Modules:
  0.0 30.3 jit_solution(7709194210121056984)
XLA Ops:
  0.6 0.0 copy-start
  1.3 2.0 %cov.1 = (bf16[256,2816]{1,0:T(8,128)(2,1)S(1)}, f32[136,128]{1,0:T(8,128)S(1)}, f32[136,128]{1,0:T(8,128)S(1)}) custom-call(s32[1,1]{1,0:T(1,128)S(6)} %copy.6.count, bf16[256,2816]{1,0:T(8,128)(2,1)} %samples.1, f32[2816]{0:T(1024)} %area.1), custom_call_target="tpu_custom_call" | custom-call | flops 369098752 | bytes 2883584 | tf_op jit(solution)/shard_map/cov/pallas_call | solution.py:258
  3.4 0.5 %collective-permute-start = (f32[136,128]{1,0:T(8,128)S(1)}, f32[136,128]{1,0:T(8,128)S(1)}, u32[]{:S(2)}, u32[]{:S(2)}) collective-permute-start(f32[136,128]{1,0:T(8,128)S(1)} %get-tuple-element.8), channel_id=1, source_target_pairs={{0,1},{1,0},{2,3},{3,2},{4,5},{5,4},{6,7},{7,6},{8,9},{9,8},{10,11... | collective-permute-start | bytes 208904 | tf_op jit(solution)/shard_map/ppermute | solution.py:241
  3.9 0.9 %collective-permute-done = f32[136,128]{1,0:T(8,128)S(1)} collective-permute-done((f32[136,128]{1,0:T(8,128)S(1)}, f32[136,128]{1,0:T(8,128)S(1)}, u32[]{:S(2)}, u32[]{:S(2)}) %collective-permute-start) | collective-permute-done | bytes 69664 | tf_op jit(solution)/shard_map/ppermute | solution.py:241
  4.8 3.9 %collective-permute-start.3 = (f32[136,128]{1,0:T(8,128)S(1)}, f32[136,128]{1,0:T(8,128)S(1)}, u32[]{:S(2)}, u32[]{:S(2)}) collective-permute-start(f32[136,128]{1,0:T(8,128)S(1)} %add.31), channel_id=1, source_target_pairs={{0,6},{1,25},{2,4},{3,27},{4,2},{5,29},{6,0},{7,31},{8,14},{9,17},... | collective-permute-start | bytes 208904 | tf_op jit(solution)/shard_map/ppermute | solution.py:241
  8.7 0.5 %collective-permute-start.2 = (f32[136,128]{1,0:T(8,128)S(1)}, f32[136,128]{1,0:T(8,128)S(1)}, u32[]{:S(2)}, u32[]{:S(2)}) collective-permute-start(f32[136,128]{1,0:T(8,128)S(1)} %add.31), channel_id=1, source_target_pairs={{0,4},{1,17},{2,6},{3,19},{4,0},{5,21},{6,2},{7,23},{8,12},{9,25},... | collective-permute-start | bytes 208904 | tf_op jit(solution)/shard_map/ppermute | solution.py:241
  9.2 0.1 collective-permute-start.1
  9.3 1.6 %collective-permute-done.3 = f32[136,128]{1,0:T(8,128)S(1)} collective-permute-done((f32[136,128]{1,0:T(8,128)S(1)}, f32[136,128]{1,0:T(8,128)S(1)}, u32[]{:S(2)}, u32[]{:S(2)}) %collective-permute-start.3) | collective-permute-done | bytes 69664 | tf_op jit(solution)/shard_map/ppermute | solution.py:241
  10.9 2.0 %collective-permute-done.2 = f32[136,128]{1,0:T(8,128)S(1)} collective-permute-done((f32[136,128]{1,0:T(8,128)S(1)}, f32[136,128]{1,0:T(8,128)S(1)}, u32[]{:S(2)}, u32[]{:S(2)}) %collective-permute-start.2) | collective-permute-done | bytes 69664 | tf_op jit(solution)/shard_map/ppermute | solution.py:241
  13.0 0.5 %collective-permute-done.1 = f32[136,128]{1,0:T(8,128)S(1)} collective-permute-done((f32[136,128]{1,0:T(8,128)S(1)}, f32[136,128]{1,0:T(8,128)S(1)}, u32[]{:S(2)}, u32[]{:S(2)}) %collective-permute-start.1) | collective-permute-done | bytes 69664 | tf_op jit(solution)/shard_map/ppermute | solution.py:241
  13.5 3.7 %collective-permute-start.6 = (f32[136,128]{1,0:T(8,128)S(1)}, f32[136,128]{1,0:T(8,128)S(1)}, u32[]{:S(2)}, u32[]{:S(2)}) collective-permute-start(f32[136,128]{1,0:T(8,128)S(1)} %add_add_fusion.1), channel_id=1, source_target_pairs={{0,24},{1,7},{2,26},{3,5},{4,28},{5,3},{6,30},{7,1},{8,16},{9,15},... | collective-permute-start | bytes 208904 | tf_op jit(solution)/shard_map/ppermute | solution.py:241
  17.2 0.0 collective-permute-start.5
  17.2 0.8 %collective-permute-start.4 = (f32[136,128]{1,0:T(8,128)S(1)}, f32[136,128]{1,0:T(8,128)S(1)}, u32[]{:S(2)}, u32[]{:S(2)}) collective-permute-start(f32[136,128]{1,0:T(8,128)S(1)} %add_add_fusion.1), channel_id=1, source_target_pairs={{0,8},{1,3},{2,10},{3,1},{4,12},{5,7},{6,14},{7,5},{8,0},{9,11},{1... | collective-permute-start | bytes 208904 | tf_op jit(solution)/shard_map/ppermute | solution.py:241
  17.9 0.0 copy-done
  17.9 0.1 compare_select_fusion.refs_2_
  18.1 1.6 %collective-permute-done.6 = f32[136,128]{1,0:T(8,128)S(1)} collective-permute-done((f32[136,128]{1,0:T(8,128)S(1)}, f32[136,128]{1,0:T(8,128)S(1)}, u32[]{:S(2)}, u32[]{:S(2)}) %collective-permute-start.6) | collective-permute-done | bytes 69664 | tf_op jit(solution)/shard_map/ppermute | solution.py:241
  19.7 2.7 %collective-permute-done.5 = f32[136,128]{1,0:T(8,128)S(1)} collective-permute-done((f32[136,128]{1,0:T(8,128)S(1)}, f32[136,128]{1,0:T(8,128)S(1)}, u32[]{:S(2)}, u32[]{:S(2)}) %collective-permute-start.5) | collective-permute-done | bytes 69664 | tf_op jit(solution)/shard_map/ppermute | solution.py:241
  22.4 0.0 collective-permute-done.4
  22.4 0.1 collective-permute-start.7
  22.5 0.9 %convolution_convert_fusion.refs_3_ = bf16[512,2816]{1,0:T(8,128)(2,1)S(1)} fusion(bf16[512,256]{1,0:T(8,128)(2,1)S(1)} %compare_select_fusion.refs_2_, bf16[256,2816]{1,0:T(8,128)(2,1)S(1)} %get-tuple-element.9), kind=kOutput, calls=%fused_computation | convolution fusion | flops 739639296 | bytes 4587520 | tf_op jit(solution)/shard_map/dot_general | solution.py:285
  23.4 0.3 %collective-permute-done.7.refs_1_ = f32[136,128]{1,0:T(8,128)S(1)} collective-permute-done((f32[136,128]{1,0:T(8,128)S(1)}, f32[136,128]{1,0:T(8,128)S(1)}, u32[]{:S(2)}, u32[]{:S(2)}) %collective-permute-start.7) | collective-permute-done | bytes 69664 | tf_op jit(solution)/shard_map/ppermute | solution.py:241
  23.7 6.6 %finish.1 = (bf16[512,2816]{1,0:T(8,128)(2,1)}, f32[512,256]{1,0:T(8,128)}) custom-call(f32[136,128]{1,0:T(8,128)S(1)} %add_add_fusion.refs_0_, f32[136,128]{1,0:T(8,128)S(1)} %collective-permute-done.7.refs_1_, bf16[512,256]{1,0:T(8,128)(2,1)S(1)} %compare_select_fusion.refs_2_, bf16[512,2816]{1,0:T(8,128)(2,1)S(1)} %convolution_convert_fusion.refs_3_), custom_call_target="tpu_custom_call" | custom-call | tf_op jit(solution)/shard_map/finish/pallas_call | solution.py:288
  (5 shorter events, 0.1 us)
Async XLA Ops:
  0.6 17.3 %copy-start = (bf16[512,256]{1,0:T(8,128)(2,1)S(1)}, bf16[512,256]{1,0:T(8,128)(2,1)}, u32[]{:S(2)}) copy-start(bf16[512,256]{1,0:T(8,128)(2,1)} %param.7) | copy-start | bytes 786436
  3.4 1.4 %collective-permute-start = (f32[136,128]{1,0:T(8,128)S(1)}, f32[136,128]{1,0:T(8,128)S(1)}, u32[]{:S(2)}, u32[]{:S(2)}) collective-permute-start(f32[136,128]{1,0:T(8,128)S(1)} %get-tuple-element.8), channel_id=1, source_target_pairs={{0,1},{1,0},{2,3},{3,2},{4,5},{5,4},{6,7},{7,6},{8,9},{9,8},{10,11... | collective-permute-start | bytes 208904 | tf_op jit(solution)/shard_map/ppermute | solution.py:241
  4.8 6.2 %collective-permute-start.3 = (f32[136,128]{1,0:T(8,128)S(1)}, f32[136,128]{1,0:T(8,128)S(1)}, u32[]{:S(2)}, u32[]{:S(2)}) collective-permute-start(f32[136,128]{1,0:T(8,128)S(1)} %add.31), channel_id=1, source_target_pairs={{0,6},{1,25},{2,4},{3,27},{4,2},{5,29},{6,0},{7,31},{8,14},{9,17},... | collective-permute-start | bytes 208904 | tf_op jit(solution)/shard_map/ppermute | solution.py:241
  8.7 4.3 %collective-permute-start.2 = (f32[136,128]{1,0:T(8,128)S(1)}, f32[136,128]{1,0:T(8,128)S(1)}, u32[]{:S(2)}, u32[]{:S(2)}) collective-permute-start(f32[136,128]{1,0:T(8,128)S(1)} %add.31), channel_id=1, source_target_pairs={{0,4},{1,17},{2,6},{3,19},{4,0},{5,21},{6,2},{7,23},{8,12},{9,25},... | collective-permute-start | bytes 208904 | tf_op jit(solution)/shard_map/ppermute | solution.py:241
  9.2 4.3 %collective-permute-start.1 = (f32[136,128]{1,0:T(8,128)S(1)}, f32[136,128]{1,0:T(8,128)S(1)}, u32[]{:S(2)}, u32[]{:S(2)}) collective-permute-start(f32[136,128]{1,0:T(8,128)S(1)} %add.31), channel_id=1, source_target_pairs={{0,2},{1,9},{2,0},{3,11},{4,6},{5,13},{6,4},{7,15},{8,10},{9,1},{1... | collective-permute-start | bytes 208904 | tf_op jit(solution)/shard_map/ppermute | solution.py:241
  13.5 6.2 %collective-permute-start.6 = (f32[136,128]{1,0:T(8,128)S(1)}, f32[136,128]{1,0:T(8,128)S(1)}, u32[]{:S(2)}, u32[]{:S(2)}) collective-permute-start(f32[136,128]{1,0:T(8,128)S(1)} %add_add_fusion.1), channel_id=1, source_target_pairs={{0,24},{1,7},{2,26},{3,5},{4,28},{5,3},{6,30},{7,1},{8,16},{9,15},... | collective-permute-start | bytes 208904 | tf_op jit(solution)/shard_map/ppermute | solution.py:241
  17.2 5.2 %collective-permute-start.5 = (f32[136,128]{1,0:T(8,128)S(1)}, f32[136,128]{1,0:T(8,128)S(1)}, u32[]{:S(2)}, u32[]{:S(2)}) collective-permute-start(f32[136,128]{1,0:T(8,128)S(1)} %add_add_fusion.1), channel_id=1, source_target_pairs={{0,16},{1,5},{2,18},{3,7},{4,20},{5,1},{6,22},{7,3},{8,24},{9,13},... | collective-permute-start | bytes 208904 | tf_op jit(solution)/shard_map/ppermute | solution.py:241
  17.2 5.2 %collective-permute-start.4 = (f32[136,128]{1,0:T(8,128)S(1)}, f32[136,128]{1,0:T(8,128)S(1)}, u32[]{:S(2)}, u32[]{:S(2)}) collective-permute-start(f32[136,128]{1,0:T(8,128)S(1)} %add_add_fusion.1), channel_id=1, source_target_pairs={{0,8},{1,3},{2,10},{3,1},{4,12},{5,7},{6,14},{7,5},{8,0},{9,11},{1... | collective-permute-start | bytes 208904 | tf_op jit(solution)/shard_map/ppermute | solution.py:241
  22.4 1.3 %collective-permute-start.7 = (f32[136,128]{1,0:T(8,128)S(1)}, f32[136,128]{1,0:T(8,128)S(1)}, u32[]{:S(2)}, u32[]{:S(2)}) collective-permute-start(f32[136,128]{1,0:T(8,128)S(1)} %add_add_fusion.refs_0_), channel_id=1, source_target_pairs={{0,1},{1,0},{2,3},{3,2},{4,5},{5,4},{6,7},{7,6},{8,9},{9,8},{10,11... | collective-permute-start | bytes 208904 | tf_op jit(solution)/shard_map/ppermute | solution.py:241

commit v5 on v4

--- a/solution.py
+++ b/solution.py
@@ -34,6 +34,13 @@
 
 def dot_nt(a, b):
     return lax.dot_general(a, b, NT, preferred_element_type=jnp.float32)
+
+
+def dot_split(a, b):
+    (a_high, a_low), (b_high, b_low) = split_bf16(a)[:2], split_bf16(b)[:2]
+    return (jnp.dot(a_high, b_low, preferred_element_type=jnp.float32)
+            + jnp.dot(a_low, b_high, preferred_element_type=jnp.float32)
+            + jnp.dot(a_high, b_high, preferred_element_type=jnp.float32))
 
 
 def chunks_of(cols, width):
@@ -208,15 +215,14 @@
         own = slice(g * WIDE, (g + 1) * WIDE)
         inverse = beside(diag, own)
         scale = (inverse * jnp.float32(total**0.5)).astype(jnp.bfloat16)
-        for start, width in chunks_of(cols, 768):
+        for start, width in chunks_of(cols, 512):
             at = slice(start, start + width)
             basis_v[own, at] = jnp.dot(
                 scale, scores[own, at], preferred_element_type=jnp.float32
             ).astype(jnp.bfloat16)
             send(basis_v, basis, (pl.ds(g * WIDE, WIDE), pl.ds(start, width)))
-        sample_v[own] = jnp.dot(
-            inverse * jnp.float32((SAMPLES / total) ** 0.5), beside(mixed_v, own),
-            precision=lax.Precision.HIGHEST, preferred_element_type=jnp.float32,
+        sample_v[own] = dot_split(
+            inverse * jnp.float32((SAMPLES / total) ** 0.5), beside(mixed_v, own)
         )
         send(sample_v, sample_basis, (pl.ds(g * WIDE, WIDE),))
     for copy in copies:

time: 30.6 us -> 30.4 us (level)
  no operation moved by 1% of the time
where the time goes in v5:
time: 30.4 us; the launch traced here: 30.2 us
  waiting for transfers between devices  9.68 us (32%)
  starting transfers between devices  9.55 us (31%)
  Pallas kernels  8.48 us (28%)
  between operations  1.37 us (5%)
  matrix products  0.91 us (3%)
    ppermute x8, waiting for transfers between devices, swap(): return lax.ppermute(value, AXES, pairs)  9.68 us
    ppermute x8, starting transfers between devices, swap(): return lax.ppermute(value, AXES, pairs)  9.55 us
    pallas_call x1, Pallas kernels, on_device(): pl.pallas_call(lambda *refs: finish_kernel(total, *refs), out_shape=(jax....  6.46 us
    pallas_call x1, Pallas kernels, on_device(): pl.pallas_call(cov_kernel, out_shape=(jax.ShapeDtypeStruct((SAMPLES, cols...  2.01 us
    dot_general x1, matrix products, on_device(): product = jnp.dot(live, weighted, preferred_element_type=jnp.float32)  0.91 us
  transfers between devices with their start and end apart: 8, of which 7 were waited for; matrix products, arithmetic and copies ran while one was open for 3% of the time, Pallas kernels for 0%

profile of v5, /device:TPU:0, one launch (start us, length us, event | category | flops | bytes accessed | tf_op | source)
XLA Modules:
  0.0 30.2 jit_solution(11384132836271075614)
XLA Ops:
  0.6 0.0 copy-start
  1.3 2.0 %cov.1 = (bf16[256,2816]{1,0:T(8,128)(2,1)S(1)}, f32[136,128]{1,0:T(8,128)S(1)}, f32[136,128]{1,0:T(8,128)S(1)}) custom-call(s32[1,1]{1,0:T(1,128)S(6)} %copy.6.count, bf16[256,2816]{1,0:T(8,128)(2,1)} %samples.1, f32[2816]{0:T(1024)} %area.1), custom_call_target="tpu_custom_call" | custom-call | flops 369098752 | bytes 2883584 | tf_op jit(solution)/shard_map/cov/pallas_call | solution.py:264
  3.4 0.5 %collective-permute-start = (f32[136,128]{1,0:T(8,128)S(1)}, f32[136,128]{1,0:T(8,128)S(1)}, u32[]{:S(2)}, u32[]{:S(2)}) collective-permute-start(f32[136,128]{1,0:T(8,128)S(1)} %get-tuple-element.8), channel_id=1, source_target_pairs={{0,1},{1,0},{2,3},{3,2},{4,5},{5,4},{6,7},{7,6},{8,9},{9,8},{10,11... | collective-permute-start | bytes 208904 | tf_op jit(solution)/shard_map/ppermute | solution.py:247
  3.9 0.9 %collective-permute-done = f32[136,128]{1,0:T(8,128)S(1)} collective-permute-done((f32[136,128]{1,0:T(8,128)S(1)}, f32[136,128]{1,0:T(8,128)S(1)}, u32[]{:S(2)}, u32[]{:S(2)}) %collective-permute-start) | collective-permute-done | bytes 69664 | tf_op jit(solution)/shard_map/ppermute | solution.py:247
  4.8 3.9 %collective-permute-start.3 = (f32[136,128]{1,0:T(8,128)S(1)}, f32[136,128]{1,0:T(8,128)S(1)}, u32[]{:S(2)}, u32[]{:S(2)}) collective-permute-start(f32[136,128]{1,0:T(8,128)S(1)} %add.31), channel_id=1, source_target_pairs={{0,6},{1,25},{2,4},{3,27},{4,2},{5,29},{6,0},{7,31},{8,14},{9,17},... | collective-permute-start | bytes 208904 | tf_op jit(solution)/shard_map/ppermute | solution.py:247
  8.7 0.5 %collective-permute-start.2 = (f32[136,128]{1,0:T(8,128)S(1)}, f32[136,128]{1,0:T(8,128)S(1)}, u32[]{:S(2)}, u32[]{:S(2)}) collective-permute-start(f32[136,128]{1,0:T(8,128)S(1)} %add.31), channel_id=1, source_target_pairs={{0,4},{1,17},{2,6},{3,19},{4,0},{5,21},{6,2},{7,23},{8,12},{9,25},... | collective-permute-start | bytes 208904 | tf_op jit(solution)/shard_map/ppermute | solution.py:247
  9.2 0.1 collective-permute-start.1
  9.3 1.6 %collective-permute-done.3 = f32[136,128]{1,0:T(8,128)S(1)} collective-permute-done((f32[136,128]{1,0:T(8,128)S(1)}, f32[136,128]{1,0:T(8,128)S(1)}, u32[]{:S(2)}, u32[]{:S(2)}) %collective-permute-start.3) | collective-permute-done | bytes 69664 | tf_op jit(solution)/shard_map/ppermute | solution.py:247
  10.9 2.0 %collective-permute-done.2 = f32[136,128]{1,0:T(8,128)S(1)} collective-permute-done((f32[136,128]{1,0:T(8,128)S(1)}, f32[136,128]{1,0:T(8,128)S(1)}, u32[]{:S(2)}, u32[]{:S(2)}) %collective-permute-start.2) | collective-permute-done | bytes 69664 | tf_op jit(solution)/shard_map/ppermute | solution.py:247
  13.0 0.5 %collective-permute-done.1 = f32[136,128]{1,0:T(8,128)S(1)} collective-permute-done((f32[136,128]{1,0:T(8,128)S(1)}, f32[136,128]{1,0:T(8,128)S(1)}, u32[]{:S(2)}, u32[]{:S(2)}) %collective-permute-start.1) | collective-permute-done | bytes 69664 | tf_op jit(solution)/shard_map/ppermute | solution.py:247
  13.5 3.7 %collective-permute-start.6 = (f32[136,128]{1,0:T(8,128)S(1)}, f32[136,128]{1,0:T(8,128)S(1)}, u32[]{:S(2)}, u32[]{:S(2)}) collective-permute-start(f32[136,128]{1,0:T(8,128)S(1)} %add_add_fusion.1), channel_id=1, source_target_pairs={{0,24},{1,7},{2,26},{3,5},{4,28},{5,3},{6,30},{7,1},{8,16},{9,15},... | collective-permute-start | bytes 208904 | tf_op jit(solution)/shard_map/ppermute | solution.py:247
  17.2 0.0 collective-permute-start.5
  17.2 0.8 %collective-permute-start.4 = (f32[136,128]{1,0:T(8,128)S(1)}, f32[136,128]{1,0:T(8,128)S(1)}, u32[]{:S(2)}, u32[]{:S(2)}) collective-permute-start(f32[136,128]{1,0:T(8,128)S(1)} %add_add_fusion.1), channel_id=1, source_target_pairs={{0,8},{1,3},{2,10},{3,1},{4,12},{5,7},{6,14},{7,5},{8,0},{9,11},{1... | collective-permute-start | bytes 208904 | tf_op jit(solution)/shard_map/ppermute | solution.py:247
  17.9 0.0 copy-done
  17.9 0.1 compare_select_fusion.refs_2_
  18.1 1.6 %collective-permute-done.6 = f32[136,128]{1,0:T(8,128)S(1)} collective-permute-done((f32[136,128]{1,0:T(8,128)S(1)}, f32[136,128]{1,0:T(8,128)S(1)}, u32[]{:S(2)}, u32[]{:S(2)}) %collective-permute-start.6) | collective-permute-done | bytes 69664 | tf_op jit(solution)/shard_map/ppermute | solution.py:247
  19.7 2.7 %collective-permute-done.5 = f32[136,128]{1,0:T(8,128)S(1)} collective-permute-done((f32[136,128]{1,0:T(8,128)S(1)}, f32[136,128]{1,0:T(8,128)S(1)}, u32[]{:S(2)}, u32[]{:S(2)}) %collective-permute-start.5) | collective-permute-done | bytes 69664 | tf_op jit(solution)/shard_map/ppermute | solution.py:247
  22.4 0.0 collective-permute-done.4
  22.4 0.1 collective-permute-start.7
  22.5 0.9 %convolution_convert_fusion.refs_3_ = bf16[512,2816]{1,0:T(8,128)(2,1)S(1)} fusion(bf16[512,256]{1,0:T(8,128)(2,1)S(1)} %compare_select_fusion.refs_2_, bf16[256,2816]{1,0:T(8,128)(2,1)S(1)} %get-tuple-element.9), kind=kOutput, calls=%fused_computation | convolution fusion | flops 739639296 | bytes 4587520 | tf_op jit(solution)/shard_map/dot_general | solution.py:291
  23.4 0.3 %collective-permute-done.7.refs_1_ = f32[136,128]{1,0:T(8,128)S(1)} collective-permute-done((f32[136,128]{1,0:T(8,128)S(1)}, f32[136,128]{1,0:T(8,128)S(1)}, u32[]{:S(2)}, u32[]{:S(2)}) %collective-permute-start.7) | collective-permute-done | bytes 69664 | tf_op jit(solution)/shard_map/ppermute | solution.py:247
  23.7 6.5 %finish.1 = (bf16[512,2816]{1,0:T(8,128)(2,1)}, f32[512,256]{1,0:T(8,128)}) custom-call(f32[136,128]{1,0:T(8,128)S(1)} %add_add_fusion.refs_0_, f32[136,128]{1,0:T(8,128)S(1)} %collective-permute-done.7.refs_1_, bf16[512,256]{1,0:T(8,128)(2,1)S(1)} %compare_select_fusion.refs_2_, bf16[512,2816]{1,0:T(8,128)(2,1)S(1)} %convolution_convert_fusion.refs_3_), custom_call_target="tpu_custom_call" | custom-call | tf_op jit(solution)/shard_map/finish/pallas_call | solution.py:294
  (5 shorter events, 0.1 us)
Async XLA Ops:
  0.6 17.3 %copy-start = (bf16[512,256]{1,0:T(8,128)(2,1)S(1)}, bf16[512,256]{1,0:T(8,128)(2,1)}, u32[]{:S(2)}) copy-start(bf16[512,256]{1,0:T(8,128)(2,1)} %param.7) | copy-start | bytes 786436
  3.4 1.4 %collective-permute-start = (f32[136,128]{1,0:T(8,128)S(1)}, f32[136,128]{1,0:T(8,128)S(1)}, u32[]{:S(2)}, u32[]{:S(2)}) collective-permute-start(f32[136,128]{1,0:T(8,128)S(1)} %get-tuple-element.8), channel_id=1, source_target_pairs={{0,1},{1,0},{2,3},{3,2},{4,5},{5,4},{6,7},{7,6},{8,9},{9,8},{10,11... | collective-permute-start | bytes 208904 | tf_op jit(solution)/shard_map/ppermute | solution.py:247
  4.8 6.2 %collective-permute-start.3 = (f32[136,128]{1,0:T(8,128)S(1)}, f32[136,128]{1,0:T(8,128)S(1)}, u32[]{:S(2)}, u32[]{:S(2)}) collective-permute-start(f32[136,128]{1,0:T(8,128)S(1)} %add.31), channel_id=1, source_target_pairs={{0,6},{1,25},{2,4},{3,27},{4,2},{5,29},{6,0},{7,31},{8,14},{9,17},... | collective-permute-start | bytes 208904 | tf_op jit(solution)/shard_map/ppermute | solution.py:247
  8.7 4.3 %collective-permute-start.2 = (f32[136,128]{1,0:T(8,128)S(1)}, f32[136,128]{1,0:T(8,128)S(1)}, u32[]{:S(2)}, u32[]{:S(2)}) collective-permute-start(f32[136,128]{1,0:T(8,128)S(1)} %add.31), channel_id=1, source_target_pairs={{0,4},{1,17},{2,6},{3,19},{4,0},{5,21},{6,2},{7,23},{8,12},{9,25},... | collective-permute-start | bytes 208904 | tf_op jit(solution)/shard_map/ppermute | solution.py:247
  9.2 4.3 %collective-permute-start.1 = (f32[136,128]{1,0:T(8,128)S(1)}, f32[136,128]{1,0:T(8,128)S(1)}, u32[]{:S(2)}, u32[]{:S(2)}) collective-permute-start(f32[136,128]{1,0:T(8,128)S(1)} %add.31), channel_id=1, source_target_pairs={{0,2},{1,9},{2,0},{3,11},{4,6},{5,13},{6,4},{7,15},{8,10},{9,1},{1... | collective-permute-start | bytes 208904 | tf_op jit(solution)/shard_map/ppermute | solution.py:247
  13.5 6.2 %collective-permute-start.6 = (f32[136,128]{1,0:T(8,128)S(1)}, f32[136,128]{1,0:T(8,128)S(1)}, u32[]{:S(2)}, u32[]{:S(2)}) collective-permute-start(f32[136,128]{1,0:T(8,128)S(1)} %add_add_fusion.1), channel_id=1, source_target_pairs={{0,24},{1,7},{2,26},{3,5},{4,28},{5,3},{6,30},{7,1},{8,16},{9,15},... | collective-permute-start | bytes 208904 | tf_op jit(solution)/shard_map/ppermute | solution.py:247
  17.2 5.2 %collective-permute-start.5 = (f32[136,128]{1,0:T(8,128)S(1)}, f32[136,128]{1,0:T(8,128)S(1)}, u32[]{:S(2)}, u32[]{:S(2)}) collective-permute-start(f32[136,128]{1,0:T(8,128)S(1)} %add_add_fusion.1), channel_id=1, source_target_pairs={{0,16},{1,5},{2,18},{3,7},{4,20},{5,1},{6,22},{7,3},{8,24},{9,13},... | collective-permute-start | bytes 208904 | tf_op jit(solution)/shard_map/ppermute | solution.py:247
  17.2 5.2 %collective-permute-start.4 = (f32[136,128]{1,0:T(8,128)S(1)}, f32[136,128]{1,0:T(8,128)S(1)}, u32[]{:S(2)}, u32[]{:S(2)}) collective-permute-start(f32[136,128]{1,0:T(8,128)S(1)} %add_add_fusion.1), channel_id=1, source_target_pairs={{0,8},{1,3},{2,10},{3,1},{4,12},{5,7},{6,14},{7,5},{8,0},{9,11},{1... | collective-permute-start | bytes 208904 | tf_op jit(solution)/shard_map/ppermute | solution.py:247
  22.4 1.3 %collective-permute-start.7 = (f32[136,128]{1,0:T(8,128)S(1)}, f32[136,128]{1,0:T(8,128)S(1)}, u32[]{:S(2)}, u32[]{:S(2)}) collective-permute-start(f32[136,128]{1,0:T(8,128)S(1)} %add_add_fusion.refs_0_), channel_id=1, source_target_pairs={{0,1},{1,0},{2,3},{3,2},{4,5},{5,4},{6,7},{7,6},{8,9},{9,8},{10,11... | collective-permute-start | bytes 208904 | tf_op jit(solution)/shard_map/ppermute | solution.py:247

commit v6 on v5

--- a/solution.py
+++ b/solution.py
@@ -49,7 +49,7 @@
 
 def cov_kernel(count, samples, area, weighted, mine, other, held, area_v, sems):
     cols = samples.shape[1]
-    parts = chunks_of(cols, 1408)
+    parts = [(0, 768), (768, cols - 768)]
     fetch = pltpu.make_async_copy(area, area_v.at[0], sems.at[len(parts)])
     fetch.start()
     copies = []
@@ -233,7 +233,7 @@
     return pl.BlockSpec(memory_space=space)
 
 
-def grid_total(mine, other):
+def grid_total(mine, other, scores):
     devices = lax.axis_size("lat") * lax.axis_size("lon")
     bits = []
     while 2 << len(bits) < devices:
@@ -254,7 +254,8 @@
             total = (total + got[0]) + (got[1] + last)
         else:
             total = total + got[0]
-    return total, swap(total, 1, 1)
+    total, scores = lax.optimization_barrier((total, scores))
+    return total, swap(total, 1, 1), scores
 
 
 def on_device(samples, area_weight, ocean_count, omega):
@@ -282,14 +283,13 @@
         pltpu.with_memory_space_constraint(area_weight, pltpu.HBM),
     )
 
-    mine, other = grid_total(mine, other)
-
     fold_row = lax.iota(jnp.int32, FOLDS * COLUMNS) // COLUMNS
     fold_col = lax.iota(jnp.int32, SAMPLES) // (SAMPLES // FOLDS)
     keeping = fold_row[:, None] != fold_col[None, :]
     live = jnp.where(keeping, omega, jnp.zeros_like(omega))
     product = jnp.dot(live, weighted, preferred_element_type=jnp.float32)
     scores = product.astype(jnp.bfloat16)
+    mine, other, scores = grid_total(mine, other, scores)
 
     point_basis, sample_basis = pl.pallas_call(
         lambda *refs: finish_kernel(total, *refs),

time: 30.4 us -> 30.4 us (level)
  no operation moved by 1% of the time
where the time goes in v6:
time: 30.4 us; the launch traced here: 30.2 us
  waiting for transfers between devices  9.68 us (32%)
  starting transfers between devices  9.55 us (31%)
  Pallas kernels  8.49 us (28%)
  between operations  1.37 us (5%)
  matrix products  0.91 us (3%)
    ppermute x8, waiting for transfers between devices, swap(): return lax.ppermute(value, AXES, pairs)  9.68 us
    ppermute x8, starting transfers between devices, swap(): return lax.ppermute(value, AXES, pairs)  9.55 us
    pallas_call x1, Pallas kernels, on_device(): pl.pallas_call(lambda *refs: finish_kernel(total, *refs), out_shape=(jax....  6.46 us
    pallas_call x1, Pallas kernels, on_device(): pl.pallas_call(cov_kernel, out_shape=(jax.ShapeDtypeStruct((SAMPLES, cols...  2.03 us
    dot_general x1, matrix products, on_device(): product = jnp.dot(live, weighted, preferred_element_type=jnp.float32)  0.91 us
  transfers between devices with their start and end apart: 8, of which 7 were waited for; matrix products, arithmetic and copies ran while one was open for 3% of the time, Pallas kernels for 0%

profile of v6, /device:TPU:0, one launch (start us, length us, event | category | flops | bytes accessed | tf_op | source)
XLA Modules:
  0.0 30.2 jit_solution(11951814711606010130)
XLA Ops:
  0.6 0.0 copy-start
  1.3 2.0 %cov.1 = (bf16[256,2816]{1,0:T(8,128)(2,1)S(1)}, f32[136,128]{1,0:T(8,128)S(1)}, f32[136,128]{1,0:T(8,128)S(1)}) custom-call(s32[1,1]{1,0:T(1,128)S(6)} %copy.6.count, bf16[256,2816]{1,0:T(8,128)(2,1)} %samples.1, f32[2816]{0:T(1024)} %area.1), custom_call_target="tpu_custom_call" | custom-call | flops 369098752 | bytes 2883584 | tf_op jit(solution)/shard_map/cov/pallas_call | solution.py:265
  3.4 0.5 %collective-permute-start = (f32[136,128]{1,0:T(8,128)S(1)}, f32[136,128]{1,0:T(8,128)S(1)}, u32[]{:S(2)}, u32[]{:S(2)}) collective-permute-start(f32[136,128]{1,0:T(8,128)S(1)} %get-tuple-element.10), channel_id=1, source_target_pairs={{0,1},{1,0},{2,3},{3,2},{4,5},{5,4},{6,7},{7,6},{8,9},{9,8},{10,11... | collective-permute-start | bytes 208904 | tf_op jit(solution)/shard_map/ppermute | solution.py:247
  3.9 0.9 %collective-permute-done = f32[136,128]{1,0:T(8,128)S(1)} collective-permute-done((f32[136,128]{1,0:T(8,128)S(1)}, f32[136,128]{1,0:T(8,128)S(1)}, u32[]{:S(2)}, u32[]{:S(2)}) %collective-permute-start) | collective-permute-done | bytes 69664 | tf_op jit(solution)/shard_map/ppermute | solution.py:247
  4.8 3.9 %collective-permute-start.3 = (f32[136,128]{1,0:T(8,128)S(1)}, f32[136,128]{1,0:T(8,128)S(1)}, u32[]{:S(2)}, u32[]{:S(2)}) collective-permute-start(f32[136,128]{1,0:T(8,128)S(1)} %add.31), channel_id=1, source_target_pairs={{0,6},{1,25},{2,4},{3,27},{4,2},{5,29},{6,0},{7,31},{8,14},{9,17},... | collective-permute-start | bytes 208904 | tf_op jit(solution)/shard_map/ppermute | solution.py:247
  8.7 0.5 %collective-permute-start.2 = (f32[136,128]{1,0:T(8,128)S(1)}, f32[136,128]{1,0:T(8,128)S(1)}, u32[]{:S(2)}, u32[]{:S(2)}) collective-permute-start(f32[136,128]{1,0:T(8,128)S(1)} %add.31), channel_id=1, source_target_pairs={{0,4},{1,17},{2,6},{3,19},{4,0},{5,21},{6,2},{7,23},{8,12},{9,25},... | collective-permute-start | bytes 208904 | tf_op jit(solution)/shard_map/ppermute | solution.py:247
  9.2 0.1 collective-permute-start.1
  9.3 0.0 copy-done
  9.3 0.1 compare_select_fusion.refs_2_
  9.5 1.5 %collective-permute-done.3 = f32[136,128]{1,0:T(8,128)S(1)} collective-permute-done((f32[136,128]{1,0:T(8,128)S(1)}, f32[136,128]{1,0:T(8,128)S(1)}, u32[]{:S(2)}, u32[]{:S(2)}) %collective-permute-start.3) | collective-permute-done | bytes 69664 | tf_op jit(solution)/shard_map/ppermute | solution.py:247
  11.0 2.0 %collective-permute-done.2 = f32[136,128]{1,0:T(8,128)S(1)} collective-permute-done((f32[136,128]{1,0:T(8,128)S(1)}, f32[136,128]{1,0:T(8,128)S(1)}, u32[]{:S(2)}, u32[]{:S(2)}) %collective-permute-start.2) | collective-permute-done | bytes 69664 | tf_op jit(solution)/shard_map/ppermute | solution.py:247
  13.0 0.5 %collective-permute-done.1 = f32[136,128]{1,0:T(8,128)S(1)} collective-permute-done((f32[136,128]{1,0:T(8,128)S(1)}, f32[136,128]{1,0:T(8,128)S(1)}, u32[]{:S(2)}, u32[]{:S(2)}) %collective-permute-start.1) | collective-permute-done | bytes 69664 | tf_op jit(solution)/shard_map/ppermute | solution.py:247
  13.5 3.7 %collective-permute-start.6 = (f32[136,128]{1,0:T(8,128)S(1)}, f32[136,128]{1,0:T(8,128)S(1)}, u32[]{:S(2)}, u32[]{:S(2)}) collective-permute-start(f32[136,128]{1,0:T(8,128)S(1)} %add_add_fusion.1), channel_id=1, source_target_pairs={{0,24},{1,7},{2,26},{3,5},{4,28},{5,3},{6,30},{7,1},{8,16},{9,15},... | collective-permute-start | bytes 208904 | tf_op jit(solution)/shard_map/ppermute | solution.py:247
  17.2 0.0 collective-permute-start.5
  17.2 0.8 %collective-permute-start.4 = (f32[136,128]{1,0:T(8,128)S(1)}, f32[136,128]{1,0:T(8,128)S(1)}, u32[]{:S(2)}, u32[]{:S(2)}) collective-permute-start(f32[136,128]{1,0:T(8,128)S(1)} %add_add_fusion.1), channel_id=1, source_target_pairs={{0,8},{1,3},{2,10},{3,1},{4,12},{5,7},{6,14},{7,5},{8,0},{9,11},{1... | collective-permute-start | bytes 208904 | tf_op jit(solution)/shard_map/ppermute | solution.py:247
  18.0 0.9 %convolution_convert_fusion.refs_3_ = bf16[512,2816]{1,0:T(8,128)(2,1)S(1)} fusion(bf16[512,256]{1,0:T(8,128)(2,1)S(1)} %compare_select_fusion.refs_2_, bf16[256,2816]{1,0:T(8,128)(2,1)S(1)} %get-tuple-element.11), kind=kOutput, calls=%fused_computation | convolution fusion | flops 739639296 | bytes 4587520 | tf_op jit(solution)/shard_map/dot_general | solution.py:290
  18.9 0.8 %collective-permute-done.6 = f32[136,128]{1,0:T(8,128)S(1)} collective-permute-done((f32[136,128]{1,0:T(8,128)S(1)}, f32[136,128]{1,0:T(8,128)S(1)}, u32[]{:S(2)}, u32[]{:S(2)}) %collective-permute-start.6) | collective-permute-done | bytes 69664 | tf_op jit(solution)/shard_map/ppermute | solution.py:247
  19.7 2.7 %collective-permute-done.5 = f32[136,128]{1,0:T(8,128)S(1)} collective-permute-done((f32[136,128]{1,0:T(8,128)S(1)}, f32[136,128]{1,0:T(8,128)S(1)}, u32[]{:S(2)}, u32[]{:S(2)}) %collective-permute-start.5) | collective-permute-done | bytes 69664 | tf_op jit(solution)/shard_map/ppermute | solution.py:247
  22.4 0.0 collective-permute-done.4
  22.4 0.1 collective-permute-start.7
  22.5 1.2 %collective-permute-done.7.refs_1_ = f32[136,128]{1,0:T(8,128)S(1)} collective-permute-done((f32[136,128]{1,0:T(8,128)S(1)}, f32[136,128]{1,0:T(8,128)S(1)}, u32[]{:S(2)}, u32[]{:S(2)}) %collective-permute-start.7) | collective-permute-done | bytes 69664 | tf_op jit(solution)/shard_map/ppermute | solution.py:247
  23.7 6.5 %finish.1 = (bf16[512,2816]{1,0:T(8,128)(2,1)}, f32[512,256]{1,0:T(8,128)}) custom-call(f32[136,128]{1,0:T(8,128)S(1)} %add_add_fusion.refs_0_, f32[136,128]{1,0:T(8,128)S(1)} %collective-permute-done.7.refs_1_, bf16[512,256]{1,0:T(8,128)(2,1)S(1)} %compare_select_fusion.refs_2_, bf16[512,2816]{1,0:T(8,128)(2,1)S(1)} %convolution_convert_fusion.refs_3_), custom_call_target="tpu_custom_call" | custom-call | tf_op jit(solution)/shard_map/finish/pallas_call | solution.py:294
  (5 shorter events, 0.1 us)
Async XLA Ops:
  0.6 8.7 %copy-start = (bf16[512,256]{1,0:T(8,128)(2,1)S(1)}, bf16[512,256]{1,0:T(8,128)(2,1)}, u32[]{:S(2)}) copy-start(bf16[512,256]{1,0:T(8,128)(2,1)} %param.7) | copy-start | bytes 786436
  3.4 1.4 %collective-permute-start = (f32[136,128]{1,0:T(8,128)S(1)}, f32[136,128]{1,0:T(8,128)S(1)}, u32[]{:S(2)}, u32[]{:S(2)}) collective-permute-start(f32[136,128]{1,0:T(8,128)S(1)} %get-tuple-element.10), channel_id=1, source_target_pairs={{0,1},{1,0},{2,3},{3,2},{4,5},{5,4},{6,7},{7,6},{8,9},{9,8},{10,11... | collective-permute-start | bytes 208904 | tf_op jit(solution)/shard_map/ppermute | solution.py:247
  4.8 6.2 %collective-permute-start.3 = (f32[136,128]{1,0:T(8,128)S(1)}, f32[136,128]{1,0:T(8,128)S(1)}, u32[]{:S(2)}, u32[]{:S(2)}) collective-permute-start(f32[136,128]{1,0:T(8,128)S(1)} %add.31), channel_id=1, source_target_pairs={{0,6},{1,25},{2,4},{3,27},{4,2},{5,29},{6,0},{7,31},{8,14},{9,17},... | collective-permute-start | bytes 208904 | tf_op jit(solution)/shard_map/ppermute | solution.py:247
  8.7 4.3 %collective-permute-start.2 = (f32[136,128]{1,0:T(8,128)S(1)}, f32[136,128]{1,0:T(8,128)S(1)}, u32[]{:S(2)}, u32[]{:S(2)}) collective-permute-start(f32[136,128]{1,0:T(8,128)S(1)} %add.31), channel_id=1, source_target_pairs={{0,4},{1,17},{2,6},{3,19},{4,0},{5,21},{6,2},{7,23},{8,12},{9,25},... | collective-permute-start | bytes 208904 | tf_op jit(solution)/shard_map/ppermute | solution.py:247
  9.2 4.3 %collective-permute-start.1 = (f32[136,128]{1,0:T(8,128)S(1)}, f32[136,128]{1,0:T(8,128)S(1)}, u32[]{:S(2)}, u32[]{:S(2)}) collective-permute-start(f32[136,128]{1,0:T(8,128)S(1)} %add.31), channel_id=1, source_target_pairs={{0,2},{1,9},{2,0},{3,11},{4,6},{5,13},{6,4},{7,15},{8,10},{9,1},{1... | collective-permute-start | bytes 208904 | tf_op jit(solution)/shard_map/ppermute | solution.py:247
  13.5 6.2 %collective-permute-start.6 = (f32[136,128]{1,0:T(8,128)S(1)}, f32[136,128]{1,0:T(8,128)S(1)}, u32[]{:S(2)}, u32[]{:S(2)}) collective-permute-start(f32[136,128]{1,0:T(8,128)S(1)} %add_add_fusion.1), channel_id=1, source_target_pairs={{0,24},{1,7},{2,26},{3,5},{4,28},{5,3},{6,30},{7,1},{8,16},{9,15},... | collective-permute-start | bytes 208904 | tf_op jit(solution)/shard_map/ppermute | solution.py:247
  17.2 5.2 %collective-permute-start.5 = (f32[136,128]{1,0:T(8,128)S(1)}, f32[136,128]{1,0:T(8,128)S(1)}, u32[]{:S(2)}, u32[]{:S(2)}) collective-permute-start(f32[136,128]{1,0:T(8,128)S(1)} %add_add_fusion.1), channel_id=1, source_target_pairs={{0,16},{1,5},{2,18},{3,7},{4,20},{5,1},{6,22},{7,3},{8,24},{9,13},... | collective-permute-start | bytes 208904 | tf_op jit(solution)/shard_map/ppermute | solution.py:247
  17.2 5.2 %collective-permute-start.4 = (f32[136,128]{1,0:T(8,128)S(1)}, f32[136,128]{1,0:T(8,128)S(1)}, u32[]{:S(2)}, u32[]{:S(2)}) collective-permute-start(f32[136,128]{1,0:T(8,128)S(1)} %add_add_fusion.1), channel_id=1, source_target_pairs={{0,8},{1,3},{2,10},{3,1},{4,12},{5,7},{6,14},{7,5},{8,0},{9,11},{1... | collective-permute-start | bytes 208904 | tf_op jit(solution)/shard_map/ppermute | solution.py:247
  22.4 1.3 %collective-permute-start.7 = (f32[136,128]{1,0:T(8,128)S(1)}, f32[136,128]{1,0:T(8,128)S(1)}, u32[]{:S(2)}, u32[]{:S(2)}) collective-permute-start(f32[136,128]{1,0:T(8,128)S(1)} %add_add_fusion.refs_0_), channel_id=1, source_target_pairs={{0,1},{1,0},{2,3},{3,2},{4,5},{5,4},{6,7},{7,6},{8,9},{9,8},{10,11... | collective-permute-start | bytes 208904 | tf_op jit(solution)/shard_map/ppermute | solution.py:247

commit v7 on v5

--- a/solution.py
+++ b/solution.py
@@ -17,6 +17,7 @@
 NT = (((1,), (1,)), ((), ()))
 VMEM = pltpu.VMEM
 SPLIT = 3
+EARLY = 512
 
 
 def iota(shape, dim):
@@ -90,7 +91,7 @@
     return jnp.take_along_axis(value, index, axis=1, mode="promise_in_bounds")
 
 
-def eliminate(rows):
+def eliminate(rows, between):
     at = iota((FOLDS, 2 * COLUMNS), 1)
     even = at < COLUMNS
     column = jnp.where(even, at, at - COLUMNS)
@@ -127,6 +128,7 @@
                 factor = pairs[q][p] if p in near else take(done[q], odd + 2 * p)
                 value = value - factor * done[q]
             rows[p] = value
+        between(j + BLOCK)
 
 
 def beside(ref, rows):
@@ -134,8 +136,9 @@
 
 
 def finish_kernel(total, mine, other, live, scores, basis, sample_basis,
-                  rows, diag, mixed_v, basis_v, sample_v, sems):
+                  rows, diag_low, diag, mixed_v, basis_v, sample_v, sems):
     cols = scores.shape[1]
+    diag_low[...] = jnp.zeros_like(diag_low)
     diag[...] = jnp.zeros_like(diag)
 
     first = lax.axis_index("lon") % 2 == 0
@@ -190,19 +193,63 @@
                 even = pltpu.roll(even, COLUMNS, 1)
             rows[:, f, :] = jnp.where(low, even, odd)
 
-    eliminate(rows)
-
-    at, pair = iota((pairs, 2 * COLUMNS), 1), iota((pairs, 2 * COLUMNS), 0)
-    for f in range(FOLDS):
-        left = f % 2 == 0
-        found = rows[:, f, :]
-        swapped = pltpu.roll(found, COLUMNS, 1)
-        column = at if left else at - COLUMNS
-        for o in (0, 1):
-            keep = (column >= 0) & (column <= 2 * pair + o)
-            value = jnp.where(keep, found if left == (o == 0) else swapped, 0.0)
-            diag[f % 4 // 2, pl.ds(f * COLUMNS + o, pairs, stride=2), :] = value
-
+    half = COLUMNS // 2
+    lanes, pair = iota((half // 2, 2 * COLUMNS), 1), iota((half // 2, 2 * COLUMNS), 0)
+    point_factor = jnp.float32(total**0.5)
+    sample_factor = jnp.float32((SAMPLES / total) ** 0.5)
+
+    def extract(target, upper, width):
+        for f in range(FOLDS):
+            tile, start = divmod(f * width % WIDE, 2 * COLUMNS)
+            found = rows[upper * half // 2 : (upper + 1) * half // 2, f, :]
+            column = lanes - start
+            for o in (0, 1):
+                shift = (start - o * COLUMNS) % (2 * COLUMNS)
+                moved = pltpu.roll(found, shift, 1) if shift else found
+                keep = (column >= 0) & (column <= 2 * pair + o + upper * half)
+                target[tile, pl.ds(f * half + o, half // 2, stride=2), :] = jnp.where(
+                    keep, moved, 0.0
+                )
+
+    def lower_rows(ref, at):
+        return jnp.concatenate(
+            [ref[f * COLUMNS : f * COLUMNS + half, at] for f in range(FOLDS)], axis=0
+        )
+
+    early = {}
+
+    def basis_early(at):
+        found = jnp.dot(
+            early["scale"], lower_rows(scores, at), preferred_element_type=jnp.float32
+        ).astype(jnp.bfloat16)
+        for f in range(FOLDS):
+            basis_v[f * COLUMNS : f * COLUMNS + half, at] = found[f * half : (f + 1) * half]
+
+    def sample_early():
+        mixed_low = jnp.concatenate(
+            [beside(mixed_v, slice(f * COLUMNS, f * COLUMNS + half)) for f in range(FOLDS)], axis=0
+        )
+        found = dot_split(early["inverse"] * sample_factor, mixed_low)
+        for f in range(FOLDS):
+            sample_v[f * COLUMNS : f * COLUMNS + half] = found[f * half : (f + 1) * half]
+
+    work = [sample_early]
+    for start, width in chunks_of(cols, EARLY):
+        work.append(lambda at=slice(start, start + width): basis_early(at))
+
+    def between(ready):
+        if ready == half:
+            extract(diag_low, 0, half)
+            early["inverse"] = beside(diag_low, slice(None))
+            early["scale"] = (early["inverse"] * point_factor).astype(jnp.bfloat16)
+        elif ready > half:
+            left = (COLUMNS - ready) // BLOCK + 1
+            for _ in range(-(-len(work) // left)):
+                work.pop(0)()
+
+    eliminate(rows, between)
+
+    extract(diag, 1, COLUMNS)
     copies = []
 
     def send(source, target, where):
@@ -213,17 +260,21 @@
 
     for g in range(FOLDS // 4):
         own = slice(g * WIDE, (g + 1) * WIDE)
-        inverse = beside(diag, own)
-        scale = (inverse * jnp.float32(total**0.5)).astype(jnp.bfloat16)
-        for start, width in chunks_of(cols, 512):
+        inverse = beside(diag, slice(g * WIDE // 2, (g + 1) * WIDE // 2))
+        scale = (inverse * point_factor).astype(jnp.bfloat16)
+        for start, width in chunks_of(cols, 768):
             at = slice(start, start + width)
-            basis_v[own, at] = jnp.dot(
+            found = jnp.dot(
                 scale, scores[own, at], preferred_element_type=jnp.float32
             ).astype(jnp.bfloat16)
+            for n in range(4):
+                row = g * WIDE + n * COLUMNS + half
+                basis_v[row : row + half, at] = found[n * half : (n + 1) * half]
             send(basis_v, basis, (pl.ds(g * WIDE, WIDE), pl.ds(start, width)))
-        sample_v[own] = dot_split(
-            inverse * jnp.float32((SAMPLES / total) ** 0.5), beside(mixed_v, own)
-        )
+        found = dot_split(inverse * sample_factor, beside(mixed_v, own))
+        for n in range(4):
+            row = g * WIDE + n * COLUMNS + half
+            sample_v[row : row + half] = found[n * half : (n + 1) * half]
         send(sample_v, sample_basis, (pl.ds(g * WIDE, WIDE),))
     for copy in copies:
         copy.wait()
@@ -301,7 +352,8 @@
         out_specs=(spec(pl.ANY), spec(pl.ANY)),
         scratch_shapes=[
             VMEM((COLUMNS // 2, FOLDS, 2 * COLUMNS), jnp.float32),
-            VMEM((2, FOLDS * COLUMNS, WIDE // 2), jnp.float32),
+            VMEM((2, FOLDS * COLUMNS // 2, WIDE // 2), jnp.float32),
+            VMEM((2, FOLDS * COLUMNS // 2, WIDE // 2), jnp.float32),
             VMEM((2, FOLDS * COLUMNS, HALF), jnp.float32),
             VMEM((FOLDS * COLUMNS, cols), jnp.bfloat16),
             VMEM((FOLDS * COLUMNS, SAMPLES), jnp.float32),

time: 30.4 us -> 30.4 us (level)
  transfers between devices with their start and end apart: 8 -> 8, of which waited for: 7 -> 7; matrix products, arithmetic and copies ran while one was open for 3% -> 4% of each run, Pallas kernels for 0% -> 0%
where the time goes in v7:
time: 30.4 us; the launch traced here: 30.1 us
  waiting for transfers between devices  9.68 us (32%)
  starting transfers between devices  9.55 us (31%)
  Pallas kernels  8.44 us (28%)
  between operations  1.37 us (5%)
  matrix products  0.91 us (3%)
    ppermute x8, waiting for transfers between devices, swap(): return lax.ppermute(value, AXES, pairs)  9.68 us
    ppermute x8, starting transfers between devices, swap(): return lax.ppermute(value, AXES, pairs)  9.55 us
    pallas_call x1, Pallas kernels, on_device(): pl.pallas_call(lambda *refs: finish_kernel(total, *refs), out_shape=(jax....  6.43 us
    pallas_call x1, Pallas kernels, on_device(): pl.pallas_call(cov_kernel, out_shape=(jax.ShapeDtypeStruct((SAMPLES, cols...  2.01 us
    dot_general x1, matrix products, on_device(): product = jnp.dot(live, weighted, preferred_element_type=jnp.float32)  0.91 us
  transfers between devices with their start and end apart: 8, of which 7 were waited for; matrix products, arithmetic and copies ran while one was open for 4% of the time, Pallas kernels for 0%

profile of v7, /device:TPU:0, one launch (start us, length us, event | category | flops | bytes accessed | tf_op | source)
XLA Modules:
  0.0 30.1 jit_solution(462773523291917469)
XLA Ops:
  0.6 0.0 copy-start
  1.3 2.0 %cov.1 = (bf16[256,2816]{1,0:T(8,128)(2,1)S(1)}, f32[136,128]{1,0:T(8,128)S(1)}, f32[136,128]{1,0:T(8,128)S(1)}) custom-call(s32[1,1]{1,0:T(1,128)S(6)} %copy.6.count, bf16[256,2816]{1,0:T(8,128)(2,1)} %samples.1, f32[2816]{0:T(1024)} %area.1), custom_call_target="tpu_custom_call" | custom-call | flops 369098752 | bytes 2883584 | tf_op jit(solution)/shard_map/cov/pallas_call | solution.py:315
  3.4 0.5 %collective-permute-start = (f32[136,128]{1,0:T(8,128)S(1)}, f32[136,128]{1,0:T(8,128)S(1)}, u32[]{:S(2)}, u32[]{:S(2)}) collective-permute-start(f32[136,128]{1,0:T(8,128)S(1)} %get-tuple-element.8), channel_id=1, source_target_pairs={{0,1},{1,0},{2,3},{3,2},{4,5},{5,4},{6,7},{7,6},{8,9},{9,8},{10,11... | collective-permute-start | bytes 208904 | tf_op jit(solution)/shard_map/ppermute | solution.py:298
  3.9 0.9 %collective-permute-done = f32[136,128]{1,0:T(8,128)S(1)} collective-permute-done((f32[136,128]{1,0:T(8,128)S(1)}, f32[136,128]{1,0:T(8,128)S(1)}, u32[]{:S(2)}, u32[]{:S(2)}) %collective-permute-start) | collective-permute-done | bytes 69664 | tf_op jit(solution)/shard_map/ppermute | solution.py:298
  4.8 3.9 %collective-permute-start.3 = (f32[136,128]{1,0:T(8,128)S(1)}, f32[136,128]{1,0:T(8,128)S(1)}, u32[]{:S(2)}, u32[]{:S(2)}) collective-permute-start(f32[136,128]{1,0:T(8,128)S(1)} %add.31), channel_id=1, source_target_pairs={{0,6},{1,25},{2,4},{3,27},{4,2},{5,29},{6,0},{7,31},{8,14},{9,17},... | collective-permute-start | bytes 208904 | tf_op jit(solution)/shard_map/ppermute | solution.py:298
  8.7 0.5 %collective-permute-start.2 = (f32[136,128]{1,0:T(8,128)S(1)}, f32[136,128]{1,0:T(8,128)S(1)}, u32[]{:S(2)}, u32[]{:S(2)}) collective-permute-start(f32[136,128]{1,0:T(8,128)S(1)} %add.31), channel_id=1, source_target_pairs={{0,4},{1,17},{2,6},{3,19},{4,0},{5,21},{6,2},{7,23},{8,12},{9,25},... | collective-permute-start | bytes 208904 | tf_op jit(solution)/shard_map/ppermute | solution.py:298
  9.2 0.1 collective-permute-start.1
  9.3 1.6 %collective-permute-done.3 = f32[136,128]{1,0:T(8,128)S(1)} collective-permute-done((f32[136,128]{1,0:T(8,128)S(1)}, f32[136,128]{1,0:T(8,128)S(1)}, u32[]{:S(2)}, u32[]{:S(2)}) %collective-permute-start.3) | collective-permute-done | bytes 69664 | tf_op jit(solution)/shard_map/ppermute | solution.py:298
  10.9 2.0 %collective-permute-done.2 = f32[136,128]{1,0:T(8,128)S(1)} collective-permute-done((f32[136,128]{1,0:T(8,128)S(1)}, f32[136,128]{1,0:T(8,128)S(1)}, u32[]{:S(2)}, u32[]{:S(2)}) %collective-permute-start.2) | collective-permute-done | bytes 69664 | tf_op jit(solution)/shard_map/ppermute | solution.py:298
  13.0 0.5 %collective-permute-done.1 = f32[136,128]{1,0:T(8,128)S(1)} collective-permute-done((f32[136,128]{1,0:T(8,128)S(1)}, f32[136,128]{1,0:T(8,128)S(1)}, u32[]{:S(2)}, u32[]{:S(2)}) %collective-permute-start.1) | collective-permute-done | bytes 69664 | tf_op jit(solution)/shard_map/ppermute | solution.py:298
  13.5 3.7 %collective-permute-start.6 = (f32[136,128]{1,0:T(8,128)S(1)}, f32[136,128]{1,0:T(8,128)S(1)}, u32[]{:S(2)}, u32[]{:S(2)}) collective-permute-start(f32[136,128]{1,0:T(8,128)S(1)} %add_add_fusion.1), channel_id=1, source_target_pairs={{0,24},{1,7},{2,26},{3,5},{4,28},{5,3},{6,30},{7,1},{8,16},{9,15},... | collective-permute-start | bytes 208904 | tf_op jit(solution)/shard_map/ppermute | solution.py:298
  17.2 0.0 collective-permute-start.5
  17.2 0.8 %collective-permute-start.4 = (f32[136,128]{1,0:T(8,128)S(1)}, f32[136,128]{1,0:T(8,128)S(1)}, u32[]{:S(2)}, u32[]{:S(2)}) collective-permute-start(f32[136,128]{1,0:T(8,128)S(1)} %add_add_fusion.1), channel_id=1, source_target_pairs={{0,8},{1,3},{2,10},{3,1},{4,12},{5,7},{6,14},{7,5},{8,0},{9,11},{1... | collective-permute-start | bytes 208904 | tf_op jit(solution)/shard_map/ppermute | solution.py:298
  17.9 0.0 copy-done
  17.9 0.1 compare_select_fusion.refs_2_
  18.1 1.6 %collective-permute-done.6 = f32[136,128]{1,0:T(8,128)S(1)} collective-permute-done((f32[136,128]{1,0:T(8,128)S(1)}, f32[136,128]{1,0:T(8,128)S(1)}, u32[]{:S(2)}, u32[]{:S(2)}) %collective-permute-start.6) | collective-permute-done | bytes 69664 | tf_op jit(solution)/shard_map/ppermute | solution.py:298
  19.7 2.7 %collective-permute-done.5 = f32[136,128]{1,0:T(8,128)S(1)} collective-permute-done((f32[136,128]{1,0:T(8,128)S(1)}, f32[136,128]{1,0:T(8,128)S(1)}, u32[]{:S(2)}, u32[]{:S(2)}) %collective-permute-start.5) | collective-permute-done | bytes 69664 | tf_op jit(solution)/shard_map/ppermute | solution.py:298
  22.4 0.0 collective-permute-done.4
  22.4 0.1 collective-permute-start.7
  22.5 0.9 %convolution_convert_fusion.refs_3_ = bf16[512,2816]{1,0:T(8,128)(2,1)S(1)} fusion(bf16[512,256]{1,0:T(8,128)(2,1)S(1)} %compare_select_fusion.refs_2_, bf16[256,2816]{1,0:T(8,128)(2,1)S(1)} %get-tuple-element.9), kind=kOutput, calls=%fused_computation | convolution fusion | flops 739639296 | bytes 4587520 | tf_op jit(solution)/shard_map/dot_general | solution.py:342
  23.4 0.3 %collective-permute-done.7.refs_1_ = f32[136,128]{1,0:T(8,128)S(1)} collective-permute-done((f32[136,128]{1,0:T(8,128)S(1)}, f32[136,128]{1,0:T(8,128)S(1)}, u32[]{:S(2)}, u32[]{:S(2)}) %collective-permute-start.7) | collective-permute-done | bytes 69664 | tf_op jit(solution)/shard_map/ppermute | solution.py:298
  23.7 6.4 %finish.1 = (bf16[512,2816]{1,0:T(8,128)(2,1)}, f32[512,256]{1,0:T(8,128)}) custom-call(f32[136,128]{1,0:T(8,128)S(1)} %add_add_fusion.refs_0_, f32[136,128]{1,0:T(8,128)S(1)} %collective-permute-done.7.refs_1_, bf16[512,256]{1,0:T(8,128)(2,1)S(1)} %compare_select_fusion.refs_2_, bf16[512,2816]{1,0:T(8,128)(2,1)S(1)} %convolution_convert_fusion.refs_3_), custom_call_target="tpu_custom_call" | custom-call | tf_op jit(solution)/shard_map/finish/pallas_call | solution.py:345
  (5 shorter events, 0.1 us)
Async XLA Ops:
  0.6 17.3 %copy-start = (bf16[512,256]{1,0:T(8,128)(2,1)S(1)}, bf16[512,256]{1,0:T(8,128)(2,1)}, u32[]{:S(2)}) copy-start(bf16[512,256]{1,0:T(8,128)(2,1)} %param.7) | copy-start | bytes 786436
  3.4 1.4 %collective-permute-start = (f32[136,128]{1,0:T(8,128)S(1)}, f32[136,128]{1,0:T(8,128)S(1)}, u32[]{:S(2)}, u32[]{:S(2)}) collective-permute-start(f32[136,128]{1,0:T(8,128)S(1)} %get-tuple-element.8), channel_id=1, source_target_pairs={{0,1},{1,0},{2,3},{3,2},{4,5},{5,4},{6,7},{7,6},{8,9},{9,8},{10,11... | collective-permute-start | bytes 208904 | tf_op jit(solution)/shard_map/ppermute | solution.py:298
  4.8 6.2 %collective-permute-start.3 = (f32[136,128]{1,0:T(8,128)S(1)}, f32[136,128]{1,0:T(8,128)S(1)}, u32[]{:S(2)}, u32[]{:S(2)}) collective-permute-start(f32[136,128]{1,0:T(8,128)S(1)} %add.31), channel_id=1, source_target_pairs={{0,6},{1,25},{2,4},{3,27},{4,2},{5,29},{6,0},{7,31},{8,14},{9,17},... | collective-permute-start | bytes 208904 | tf_op jit(solution)/shard_map/ppermute | solution.py:298
  8.7 4.3 %collective-permute-start.2 = (f32[136,128]{1,0:T(8,128)S(1)}, f32[136,128]{1,0:T(8,128)S(1)}, u32[]{:S(2)}, u32[]{:S(2)}) collective-permute-start(f32[136,128]{1,0:T(8,128)S(1)} %add.31), channel_id=1, source_target_pairs={{0,4},{1,17},{2,6},{3,19},{4,0},{5,21},{6,2},{7,23},{8,12},{9,25},... | collective-permute-start | bytes 208904 | tf_op jit(solution)/shard_map/ppermute | solution.py:298
  9.2 4.3 %collective-permute-start.1 = (f32[136,128]{1,0:T(8,128)S(1)}, f32[136,128]{1,0:T(8,128)S(1)}, u32[]{:S(2)}, u32[]{:S(2)}) collective-permute-start(f32[136,128]{1,0:T(8,128)S(1)} %add.31), channel_id=1, source_target_pairs={{0,2},{1,9},{2,0},{3,11},{4,6},{5,13},{6,4},{7,15},{8,10},{9,1},{1... | collective-permute-start | bytes 208904 | tf_op jit(solution)/shard_map/ppermute | solution.py:298
  13.5 6.2 %collective-permute-start.6 = (f32[136,128]{1,0:T(8,128)S(1)}, f32[136,128]{1,0:T(8,128)S(1)}, u32[]{:S(2)}, u32[]{:S(2)}) collective-permute-start(f32[136,128]{1,0:T(8,128)S(1)} %add_add_fusion.1), channel_id=1, source_target_pairs={{0,24},{1,7},{2,26},{3,5},{4,28},{5,3},{6,30},{7,1},{8,16},{9,15},... | collective-permute-start | bytes 208904 | tf_op jit(solution)/shard_map/ppermute | solution.py:298
  17.2 5.2 %collective-permute-start.5 = (f32[136,128]{1,0:T(8,128)S(1)}, f32[136,128]{1,0:T(8,128)S(1)}, u32[]{:S(2)}, u32[]{:S(2)}) collective-permute-start(f32[136,128]{1,0:T(8,128)S(1)} %add_add_fusion.1), channel_id=1, source_target_pairs={{0,16},{1,5},{2,18},{3,7},{4,20},{5,1},{6,22},{7,3},{8,24},{9,13},... | collective-permute-start | bytes 208904 | tf_op jit(solution)/shard_map/ppermute | solution.py:298
  17.2 5.2 %collective-permute-start.4 = (f32[136,128]{1,0:T(8,128)S(1)}, f32[136,128]{1,0:T(8,128)S(1)}, u32[]{:S(2)}, u32[]{:S(2)}) collective-permute-start(f32[136,128]{1,0:T(8,128)S(1)} %add_add_fusion.1), channel_id=1, source_target_pairs={{0,8},{1,3},{2,10},{3,1},{4,12},{5,7},{6,14},{7,5},{8,0},{9,11},{1... | collective-permute-start | bytes 208904 | tf_op jit(solution)/shard_map/ppermute | solution.py:298
  22.4 1.3 %collective-permute-start.7 = (f32[136,128]{1,0:T(8,128)S(1)}, f32[136,128]{1,0:T(8,128)S(1)}, u32[]{:S(2)}, u32[]{:S(2)}) collective-permute-start(f32[136,128]{1,0:T(8,128)S(1)} %add_add_fusion.refs_0_), channel_id=1, source_target_pairs={{0,1},{1,0},{2,3},{3,2},{4,5},{5,4},{6,7},{7,6},{8,9},{9,8},{10,11... | collective-permute-start | bytes 208904 | tf_op jit(solution)/shard_map/ppermute | solution.py:298
